TPU v7x, 32 devices: a whole 2x2x4 slice. The times are simulated.
32 devices in a mesh: regime: 2 (over y), obj: 16 (over z, x, core).
Axes of the slice: x: 2, y: 2, z: 4, core: 2. Of those that a mesh axis runs over, the one named last changes fastest.
Arguments:
- local_jac: bfloat16 [7, 15360], P(None, ('regime', 'obj')), may hold values from -6 to 6
- global_jac: bfloat16 [15360, 512], P(('regime', 'obj')), may hold values from -0.5325352 to 0.5325352
- coeff_index: int32 [4, 15360], P(None, ('regime', 'obj')), may hold values from 0 to 511
- coeff_weight: bfloat16 [4, 15360], P(None, ('regime', 'obj')), may hold values from -4.131182 to 4.131182
- residual: float32 [15360], P(('regime', 'obj')), may hold values from -10 to 10
- obs_weight: float32 [15360], P(('regime', 'obj')), may hold values from 0.3 to 3
- obs_count: int32 [256], P(('regime', 'obj')), may hold values from 1 to 60
- local_prior: float32 [7, 256], P(None, ('regime', 'obj')), may hold values from 0.3 to 3
- regional_prior: float32 [2, 512], P('regime'), may hold values from 0.1 to 1
- global_prior: float32 [512], replicated, may hold values from 0.3 to 3
Outputs:
- local_step: float32 [7, 256], P(None, ('regime', 'obj'))
- regional_step: float32 [2, 512], P('regime')
- global_step: float32 [512], replicated
All inputs are finite; a program needn't handle non-finite values.
Results may differ from a plain program's by a relative error of at most 0.0005.
The roundings to bfloat16 on the way count: a program that leaves them out, or rounds other values in their place, can miss the bound.
Values sent between devices are 32-bit elements; how exact they have to be, the bound alone decides.
A program may use at most 64 MiB of HBM per device.

v0:
```python
import jax
import jax.numpy as jnp
from jax import lax
from jax.experimental import pallas as pl
from jax.experimental.pallas import tpu as pltpu
from jax.sharding import PartitionSpec as P


def live_weight(obs_weight, obs_count, observed):
    objects = obs_count.shape[0]
    position = jnp.arange(observed, dtype=jnp.int32)
    present = (position[None, :] < obs_count[:, None]).reshape(objects * observed)
    return (jnp.where(present, obs_weight, jnp.float32(0.0)), present)


def jacobian(coeff_index, coeff_weight, global_jac, regional_width):
    columns = jnp.arange(regional_width, dtype=jnp.int32)
    regional = jnp.zeros((coeff_index.shape[1], regional_width), jnp.float32)
    for k in range(coeff_index.shape[0]):
        regional = regional + jnp.where(
            coeff_index[k][:, None] == columns[None, :],
            coeff_weight[k][:, None].astype(jnp.float32),
            jnp.float32(0.0),
        )
    return jnp.concatenate([regional.astype(jnp.bfloat16), global_jac], axis=1)


def cholesky_small(entries):
    order = len(entries)
    factor = [[None] * order for i in range(order)]
    for j in range(order):
        diagonal = entries[j][j]
        for k in range(j):
            diagonal = diagonal - factor[j][k] * factor[j][k]
        factor[j][j] = jnp.sqrt(diagonal)
        for i in range(j + 1, order):
            current = entries[i][j]
            for k in range(j):
                current = current - factor[i][k] * factor[j][k]
            factor[i][j] = current / factor[j][j]
    return factor


def broaden(entry, like):
    return entry.reshape(entry.shape + (1,) * (like.ndim - 1))


def forward_small(factor, target):
    result = []
    for a in range(len(target)):
        current = target[a]
        for k in range(a):
            current = current - broaden(factor[a][k], current) * result[k]
        result.append(current / broaden(factor[a][a], current))
    return result


def backward_small(factor, target):
    order = len(target)
    result = [None] * order
    for a in reversed(range(order)):
        current = target[a]
        for k in range(a + 1, order):
            current = current - broaden(factor[k][a], current) * result[k]
        result[a] = current / broaden(factor[a][a], current)
    return result


PANEL = 128
GROUP = 8
FULL = lax.Precision.HIGHEST


def inverse_factor(block):
    order = block.shape[0]
    lane = lax.broadcasted_iota(jnp.int32, (GROUP, order), 1)
    sub = lax.broadcasted_iota(jnp.int32, (GROUP, order), 0)
    shape = (GROUP, order)
    chunks = [block[i * GROUP : (i + 1) * GROUP, :] for i in range(order // GROUP)]
    for g in range(order // GROUP):
        base = g * GROUP
        inside = (lane >= base) & (lane < base + GROUP)
        cols = {
            i: [jnp.broadcast_to(chunks[i][:, base + b : base + b + 1], shape) for b in range(GROUP)]
            for i in range(g, len(chunks))
        }
        small = [
            [jnp.broadcast_to(cols[g][b][a : a + 1, :], shape) if a >= b else None for b in range(GROUP)]
            for a in range(GROUP)
        ]
        rows = [
            jnp.where(
                lane == base + b,
                jnp.float32(1.0),
                jnp.where(inside, jnp.float32(0.0), jnp.broadcast_to(chunks[g][b : b + 1, :], shape)),
            )
            for b in range(GROUP)
        ]
        inverse = []
        for b in range(GROUP):
            recip = 1.0 / small[b][b]
            inverse.append(recip)
            ratio = [small[a][b] * recip if a > b else None for a in range(GROUP)]
            for a in range(b + 1, GROUP):
                rows[a] = rows[a] - ratio[a] * rows[b]
                for c in range(b + 1, a + 1):
                    small[a][c] = small[a][c] - ratio[a] * small[c][b]
            for i in range(g + 1, len(chunks)):
                for c in range(b + 1, GROUP):
                    cols[i][c] = cols[i][c] - cols[i][b] * ratio[c]
        scaled_rows = [rows[b] * inverse[b] for b in range(GROUP)]
        for i in range(g + 1, len(chunks)):
            current = jnp.where(inside, jnp.float32(0.0), chunks[i])
            for b in range(GROUP):
                current = current - cols[i][b] * scaled_rows[b]
            chunks[i] = current
        final = jnp.zeros(shape, jnp.float32)
        for b in range(GROUP):
            final = jnp.where(sub == b, rows[b] / jnp.sqrt(small[b][b]), final)
        chunks[g] = jnp.where(lane <= sub + base, final, jnp.float32(0.0))
    return jnp.concatenate(chunks, axis=0)


def dot_tn(left, right):
    return lax.dot_general(left, right, (((0,), (0,)), ((), ())), precision=FULL, preferred_element_type=jnp.float32)


def dot_nt(left, right):
    return lax.dot_general(left, right, (((1,), (1,)), ((), ())), precision=FULL, preferred_element_type=jnp.float32)


def dot_nn(left, right):
    return lax.dot_general(left, right, (((1,), (0,)), ((), ())), precision=FULL, preferred_element_type=jnp.float32)


def eliminate(work, inv, y):
    order = work.shape[0]
    count = order // PANEL

    def panel(p, carry):
        for q in range(1, count):
            @pl.when(p == q)
            def update(q=q):
                at = q * PANEL
                above = work[0:at, at : at + PANEL]
                work[at : at + PANEL, at:] = work[at : at + PANEL, at:] - dot_tn(above, work[0:at, at:])
                y[:, at : at + PANEL] = y[:, at : at + PANEL] - dot_nn(y[:, 0:at], above)

        at = pl.multiple_of(p * PANEL, PANEL)
        inv[pl.ds(at, PANEL), :] = inverse_factor(work[pl.ds(at, PANEL), pl.ds(at, PANEL)])
        for q in range(count):
            @pl.when(p == q)
            def apply(q=q):
                at = q * PANEL
                own = inv[at : at + PANEL, :]
                if at + PANEL < work.shape[1]:
                    work[at : at + PANEL, at + PANEL :] = dot_nn(own, work[at : at + PANEL, at + PANEL :])
                y[:, at : at + PANEL] = dot_nt(y[:, at : at + PANEL], own)

        return carry

    lax.fori_loop(0, count, panel, 0)


def back_substitute(work, inv, y):
    order = work.shape[0]
    for q in reversed(range(order // PANEL)):
        at = q * PANEL
        current = y[:, at : at + PANEL]
        if at + PANEL < order:
            current = current - dot_nt(y[:, at + PANEL : order], work[at : at + PANEL, at + PANEL : order])
        y[:, at : at + PANEL] = dot_nn(current, inv[at : at + PANEL, :])


def add_diagonal(work, prior, damping):
    order = work.shape[0]
    for q in range(order // PANEL):
        at = q * PANEL
        rows = lax.broadcasted_iota(jnp.int32, (PANEL, PANEL), 0)
        columns = lax.broadcasted_iota(jnp.int32, (PANEL, PANEL), 1)
        extra = jnp.broadcast_to(prior[0:1, at : at + PANEL] * damping, (PANEL, PANEL))
        tile = work[at : at + PANEL, at : at + PANEL]
        work[at : at + PANEL, at : at + PANEL] = tile + jnp.where(rows == columns, extra, jnp.float32(0.0))


def regional_kernel(damping, square, block, vector, prior, work, inv, y, gram, gram_vector):
    width = square.shape[0]
    work[:, 0:width] = square[...]
    work[:, width:] = block[...]
    add_diagonal(work, prior, damping[0])
    y[...] = jnp.broadcast_to(vector[...], y.shape)
    eliminate(work, inv, y)
    gram[...] = dot_tn(work[:, width:], work[:, width:])
    gram_vector[...] = dot_nn(y[...], work[:, width:])[0:1, :]


def final_kernel(damping, matrix, vector, prior, work, inv, y, global_step, regional_step, gwork, ginv, gy, ry):
    width = work.shape[0]
    gwork[...] = matrix[...]
    add_diagonal(gwork, prior, damping[0])
    gy[...] = jnp.broadcast_to(vector[...], gy.shape)
    eliminate(gwork, ginv, gy)
    back_substitute(gwork, ginv, gy)
    global_step[...] = gy[0:1, :]
    ry[...] = y[...] - dot_nt(gy[...], work[:, width:])
    back_substitute(work, inv, ry)
    regional_step[...] = ry[0:1, :]


def vmem(count):
    return [pl.BlockSpec(memory_space=pltpu.VMEM)] * count


def regional_eliminate(damping, square, block, vector, prior):
    width, extra = block.shape
    f32 = jnp.float32
    return pl.pallas_call(
        regional_kernel,
        out_shape=(
            jax.ShapeDtypeStruct((width, width + extra), f32),
            jax.ShapeDtypeStruct((width, PANEL), f32),
            jax.ShapeDtypeStruct((8, width), f32),
            jax.ShapeDtypeStruct((extra, extra), f32),
            jax.ShapeDtypeStruct((1, extra), f32),
        ),
        in_specs=[pl.BlockSpec(memory_space=pltpu.SMEM)] + vmem(4),
        out_specs=tuple(vmem(5)),
        cost_estimate=pl.CostEstimate(flops=30000000000, bytes_accessed=8000000, transcendentals=0),
        name="regional",
    )(damping, square, block, vector, prior)


def final_solve(damping, matrix, vector, prior, work, inv, y):
    order, width = matrix.shape[0], work.shape[0]
    f32 = jnp.float32
    return pl.pallas_call(
        final_kernel,
        out_shape=(jax.ShapeDtypeStruct((1, order), f32), jax.ShapeDtypeStruct((1, width), f32)),
        in_specs=[pl.BlockSpec(memory_space=pltpu.SMEM)] + vmem(6),
        out_specs=tuple(vmem(2)),
        scratch_shapes=[
            pltpu.VMEM((order, order), f32),
            pltpu.VMEM((order, PANEL), f32),
            pltpu.VMEM((8, order), f32),
            pltpu.VMEM((8, width), f32),
        ],
        name="final",
    )(damping, matrix, vector, prior, work, inv, y)


def body(
    local_jac,
    global_jac,
    coeff_index,
    coeff_weight,
    residual,
    obs_weight,
    obs_count,
    local_prior,
    regional_prior,
    global_prior,
):
    objects = obs_count.shape[0]
    observed = local_jac.shape[1] // objects
    nparams = local_jac.shape[0]
    regional_width = regional_prior.shape[1]
    weight, present = live_weight(obs_weight, obs_count, observed)
    misfit, counted = lax.psum(
        (jnp.sum(weight * residual * residual), jnp.sum(present.astype(jnp.float32))),
        ("regime", "obj"),
    )
    damping = misfit / counted
    joined = jacobian(coeff_index, coeff_weight, global_jac, regional_width)
    scaled = (joined.astype(jnp.float32) * weight[:, None]).astype(jnp.bfloat16)
    normal = jnp.dot(scaled.T, joined, preferred_element_type=jnp.float32)
    gradient = jnp.dot(residual, scaled.astype(jnp.float32), precision=lax.Precision.HIGHEST)
    local_rows = local_jac.astype(jnp.float32).reshape(nparams, objects, observed)
    weighted_local = local_rows * weight.reshape(objects, observed)[None]
    small_normal = jnp.einsum(
        "anp,bnp->abn", weighted_local, local_rows, precision=lax.Precision.HIGHEST
    )
    entries = [
        [small_normal[a, b] + (local_prior[a] if a == b else 0.0) for b in range(nparams)]
        for a in range(nparams)
    ]
    factor = cholesky_small(entries)
    coupling = jnp.einsum(
        "anp,npc->anc",
        weighted_local,
        joined.reshape(objects, observed, -1).astype(jnp.float32),
        precision=lax.Precision.HIGHEST,
    )
    local_gradient = jnp.sum(weighted_local * residual.reshape(objects, observed)[None], axis=2)
    reduced = forward_small(factor, [coupling[a] for a in range(nparams)])
    reduced_gradient = forward_small(factor, [local_gradient[a] for a in range(nparams)])
    stacked = jnp.concatenate(reduced, axis=0)
    vector = jnp.concatenate(reduced_gradient, axis=0)
    schur = normal - jnp.dot(stacked.T, stacked, precision=lax.Precision.HIGHEST)
    rhs = gradient - jnp.dot(vector, stacked, precision=lax.Precision.HIGHEST)
    width = regional_width
    upper = jnp.concatenate([schur[:width], rhs.reshape(1, -1)], axis=0)
    upper = lax.psum(upper, "obj")
    damp = damping.reshape(1)
    regional_block, block = upper[:width, :width], upper[:width, width:]
    rhs_regional, rhs_global = upper[width:, :width], upper[width:, width:]
    global_block = lax.psum(schur[width:, width:], ("regime", "obj"))
    regional_block = 0.5 * (regional_block + regional_block.T)
    global_block = 0.5 * (global_block + global_block.T)
    work, inverse, y, gram, gram_vector = regional_eliminate(
        damp, regional_block, block, rhs_regional, regional_prior
    )
    reduced_global = jnp.concatenate([-gram, rhs_global - gram_vector], axis=0)
    reduced_global = lax.psum(reduced_global, "regime")
    global_step, regional_step = final_solve(
        damp,
        global_block + reduced_global[:-1],
        reduced_global[-1:],
        global_prior[None, :],
        work,
        inverse,
        y,
    )
    global_step, regional_step = global_step[0], regional_step[0]
    update = jnp.concatenate([regional_step, global_step], axis=0)
    moved = jnp.dot(joined.astype(jnp.float32), update, precision=lax.Precision.HIGHEST)
    target = jnp.sum(weighted_local * (residual - moved).reshape(objects, observed)[None], axis=2)
    solved = backward_small(factor, forward_small(factor, [target[a] for a in range(nparams)]))
    local_step = jnp.stack(solved, axis=0)
    return (local_step, regional_step[None, :], global_step)


def solution(mesh):
    return jax.shard_map(
        body,
        mesh=mesh,
        in_specs=(
            P(None, ("regime", "obj")),
            P(("regime", "obj"), None),
            P(None, ("regime", "obj")),
            P(None, ("regime", "obj")),
            P(("regime", "obj")),
            P(("regime", "obj")),
            P(("regime", "obj")),
            P(None, ("regime", "obj")),
            P("regime", None),
            P(),
        ),
        out_specs=(P(None, ("regime", "obj")), P("regime", None), P()),
        check_vma=False,
    )
```

profile of v0, /device:TPU:0, one launch (start us, length us, event | category | flops | bytes accessed | tf_op | source)
XLA Modules:
  0.0 352.3 jit_solution(16580492543332107553)
XLA Ops:
  7.2 0.7 iota_compare_fusion.4
  8.0 1.3 fusion.39
  9.4 0.8 reshape.1572
  10.4 0.3 slice_reduce_fusion.11
  10.7 0.5 slice_reduce_fusion.8
  11.1 0.8 mul.2432
  12.0 0.3 slice_reduce_fusion
  12.3 0.9 fusion.77
  13.1 0.8 slice_convert_fusion.3
  14.0 0.8 add_convert_fusion
  14.7 1.1 pad_maximum_fusion.2
  15.9 0.2 reshape.1575
  16.1 0.5 convolution_bitcast_fusion
  16.6 0.2 fusion.75
  17.6 0.2 fusion.31
  17.8 3.5 %fusion.79 = f32[1024,1024]{0,1:T(8,128)S(1)} fusion(f32[56,1024]{1,0:T(8,128)S(1)} %fusion.31), kind=kOutput, calls=%fused_computation.239 | convolution fusion | flops 704643072 | bytes 4423680 | tf_op jit(solution)/shard_map/dot_general | solution.py:298
  21.4 1.4 convolution_subtract_fusion
  22.9 0.2 slice.324
  23.1 1.7 copy-done
  24.8 0.2 fusion.52
  25.1 0.6 fusion
  25.7 1.0 copy.171
  26.7 2.8 pad_maximum_fusion
  29.6 2.3 slice.323
  31.9 0.7 convert_reduce_fusion
  32.6 42.6 %all-reduce = (f32[]{:T(128)}, f32[]{:T(128)}) all-reduce(f32[]{:T(128)} %get-tuple-element.151, f32[]{:T(128)} %convert_reduce_fusion), channel_id=1, replica_groups=mesh['regime'=2,'obj'=16] {'regime','obj'}, use_global_device_ids=true, to_apply=%region_1.2 | all-reduce | flops 2 | bytes 16 | tf_op jit(solution)/shard_map/psum | solution.py:268
  76.6 57.1 %all-reduce.7.cloned.1.call-done = f32[513,1024]{0,1:T(8,128)} async-done(((f32[513,1024]{0,1:T(8,128)}), f32[513,1024]{0,1:T(8,128)}) %all-reduce.7.cloned.1.call-update) | async-done | bytes 2101264 | tf_op jit(solution)/shard_map/psum | solution.py:302
  133.7 2.7 fusion.74
  136.4 1.6 copy.172
  138.0 1.3 copy.173.block
  139.3 1.1 fusion.73
  140.4 0.7 copy.174.vector
  141.1 2.4 fusion.1.square
  143.5 27.3 %regional.1 = (f32[512,1024]{1,0:T(8,128)}, f32[512,128]{1,0:T(8,128)}, f32[8,512]{1,0:T(8,128)}, f32[512,512]{1,0:T(8,128)}, f32[1,512]{1,0:T(1,128)}) custom-call(f32[1]{0:T(128)} %bitcast.8.damping, f32[512,512]{1,0:T(8,128)} %fusion.1.square, f32[512,512]{1,0:T(8,128)} %copy.173.block, f32[1,512]{1,0:T(1,128)} %copy.174.vector, f32[1,512]{1,0:T(1,128)} %prior.1), custom_call_target="tpu_custom_call" | custom-call | flops 30000001024 | bytes 8000000 | tf_op jit(solution)/shard_map/regional/pallas_call | solution.py:217
  170.8 1.3 neg.3
  172.3 1.1 pad_maximum_fusion.1
  173.9 0.2 fusion.76
  174.1 95.3 %all-reduce.5.cloned.1.call-done = f32[512,512]{0,1:T(8,128)} async-done(((f32[512,512]{0,1:T(8,128)}), f32[512,512]{0,1:T(8,128)}) %all-reduce.5.cloned.1.call-update) | async-done | bytes 1048592 | tf_op jit(solution)/shard_map/psum | solution.py:306
  269.4 2.6 copy.169
  272.1 1.4 bitcast_add_fusion.1
  273.5 0.3 copy.170
  273.8 37.4 %all-reduce.9.cloned.1.call-done = f32[513,512]{1,0:T(8,128)} async-done(((f32[513,512]{1,0:T(8,128)}), f32[513,512]{1,0:T(8,128)}) %all-reduce.9.cloned.1.call-update) | async-done | bytes 1050640 | tf_op jit(solution)/shard_map/psum | solution.py:313
  311.2 1.3 slice.330.vector
  312.5 2.4 slice_add_fusion.matrix
  314.9 28.0 %final.1 = (f32[1,512]{1,0:T(1,128)}, f32[1,512]{1,0:T(1,128)}) custom-call(f32[1]{0:T(128)} %bitcast.8.damping, f32[512,512]{1,0:T(8,128)} %slice_add_fusion.matrix, f32[1,512]{1,0:T(1,128)} %slice.330.vector, f32[1,512]{1,0:T(1,128)} %bitcast.324, f32[512,1024]{1,0:T(8,128)} %get-tuple-element.12.work, f32[512,128]{1,0:T(8,128)} %get-tuple-element.13.inv, ...), custom_call_target="tpu_custom_call" | custom-call | tf_op jit(solution)/shard_map/final/pallas_call | solution.py:236
  342.9 0.7 pad_maximum_fusion.3
  343.6 0.9 fusion.80
  345.1 0.7 copy.204
  (55 shorter events, 2.8 us)
Async XLA Ops:
  7.2 126.6 %all-reduce.7.cloned.1.call-start = ((), (), s32[]{:S(2)}) async-start(), calls=%async_computation.1 | async-start | bytes 5242880 | tf_op jit(solution)/shard_map/psum | solution.py:302
  15.9 0.9 copy-start.3
  22.8 1.9 copy-start
  22.8 2.2 copy-start.2
  29.5 2.4 copy-start.5
  29.5 239.9 %all-reduce.5.cloned.1.call-start = ((), (), s32[]{:S(2)}) async-start(), calls=%async_computation | async-start | bytes 2097152 | tf_op jit(solution)/shard_map/psum | solution.py:306
  31.9 279.3 %all-reduce.9.cloned.1.call-start = ((), (), s32[]{:S(2)}) async-start(), calls=%async_computation.2 | async-start | bytes 2129920 | tf_op jit(solution)/shard_map/psum | solution.py:313
  170.8 1.4 copy-start.4
  269.4 2.6 copy-start.1
Sparse Core Ops, SparseCore 0:
  29.7 104.0 all-reduce.6
  138.9 130.4 all-reduce.4
  271.7 39.4 all-reduce.8
where the time goes:
time: 353 us; the launch traced here: 352 us
  waiting for transfers between devices  190 us (54%)
  Pallas kernels  55.3 us (16%)
  blocking collectives  42.6 us (12%)
  local copies, waits for them, and re-layouts  22.6 us (6%)
  other arithmetic  19.1 us (5%)
  between operations  15.4 us (4%)
  matrix products  7.32 us (2%)
    psum x1, waiting for transfers between devices, body(): global_block = lax.psum(schur[width:, width:], ('regime', 'obj'))  95.3 us
    psum x1, waiting for transfers between devices, body(): upper = lax.psum(upper, 'obj')  57.1 us
    psum x1, blocking collectives, body(): lax.psum((jnp.sum(weight * residual * residual), jnp.sum(present.astype(j...  42.6 us
    psum x1, waiting for transfers between devices, body(): reduced_global = lax.psum(reduced_global, 'regime')  37.4 us
    pallas_call x1, Pallas kernels, final_solve(): pl.pallas_call(final_kernel, out_shape=(jax.ShapeDtypeStruct((1, order),...  28 us
    pallas_call x1, Pallas kernels, regional_eliminate(): pl.pallas_call(regional_kernel, out_shape=(jax.ShapeDtypeStruct((width, w...  27.3 us
  transfers between devices with their start and end apart: 3, of which 3 were waited for; matrix products, arithmetic and copies ran while one was open for 6% of the time, Pallas kernels for 8%

commit v1 on v0

v1 whole, which is shorter than its diff:
```python
import functools

import jax
import jax.numpy as jnp
from jax import lax
from jax.experimental import pallas as pl
from jax.experimental.pallas import tpu as pltpu
from jax.sharding import PartitionSpec as P

PANEL = 128
GROUP = 8
FULL = lax.Precision.HIGHEST
F32 = jnp.float32
BF16 = jnp.bfloat16
MESH = pl.DeviceIdType.MESH


def dot(left, right, contract, precision=None):
    return lax.dot_general(
        left, right, ((contract[:1], contract[1:]), ((), ())), precision=precision, preferred_element_type=F32
    )


def dot_tn(left, right, precision=FULL):
    return dot(left, right, (0, 0), precision)


def dot_nt(left, right, precision=FULL):
    return dot(left, right, (1, 1), precision)


def dot_nn(left, right, precision=FULL):
    return dot(left, right, (1, 0), precision)


def tiles_upper(count):
    return [(i, j) for i in range(count) for j in range(i, count)]


def stage_plan(count):
    plan, stride = [], 1
    while stride < count:
        left = count // stride
        if stride < 4 and left % 2 == 0:
            radix = 2
        elif left % 4 == 0:
            radix = 4
        else:
            radix = left
        plan.append((radix, stride))
        stride *= radix
    return tuple(plan)


def padded(rows, count):
    unit = GROUP * count
    return -(-rows // unit) * unit


def digit_of(o, radix, stride):
    return lax.rem(lax.div(o, stride), radix)


def peer_of(o, radix, stride, k):
    digit = digit_of(o, radix, stride)
    other = lax.rem(digit + k + 1, radix)
    return o + (other - digit) * stride, digit, other


def owned_base(o, rows, plan):
    base, size = 0, rows
    for radix, stride in plan:
        size = size // radix
        base = base + digit_of(o, radix, stride) * size
    return base


def enter(plan, n_regime):
    r, o = lax.axis_index("regime"), lax.axis_index("obj")
    barrier = pltpu.get_barrier_semaphore()
    total = 0
    for radix, stride in plan:
        for k in range(radix - 1):
            pl.semaphore_signal(barrier, inc=1, device_id=(r, peer_of(o, radix, stride, k)[0]), device_id_type=MESH)
            total += 1
    for k in range(n_regime - 1):
        pl.semaphore_signal(barrier, inc=1, device_id=(lax.rem(r + k + 1, n_regime), o), device_id_type=MESH)
        total += 1
    return barrier, total


class Section:
    def __init__(self, rows, plan, part, recv, full, sems):
        self.rows, self.plan = rows, plan
        self.part, self.recv, self.full = part, recv, full
        self.scatter_send, self.scatter_recv, self.gather_send, self.gather_recv = sems
        self.r, self.o = lax.axis_index("regime"), lax.axis_index("obj")
        self.base, self.size, self.used = 0, rows, 0
        self.flight = []

    def rows_at(self, base, size):
        return pl.ds(pl.multiple_of(base, GROUP) if not isinstance(base, int) else base, size)

    def scatter_start(self, stage):
        radix, stride = self.plan[stage]
        self.sub = self.size // radix
        self.flight = []
        for k in range(radix - 1):
            to, digit, other = peer_of(self.o, radix, stride, k)
            copy = pltpu.make_async_remote_copy(
                src_ref=self.part.at[self.rows_at(self.base + other * self.sub, self.sub)],
                dst_ref=self.recv.at[pl.ds(self.used + k * self.sub, self.sub)],
                send_sem=self.scatter_send.at[stage, k],
                recv_sem=self.scatter_recv.at[stage, k],
                device_id=(self.r, to),
                device_id_type=MESH,
            )
            copy.start()
            self.flight.append(copy)

    def scatter_finish(self, stage, target=None):
        radix, stride = self.plan[stage]
        for copy in self.flight:
            copy.wait()
        base = self.base + digit_of(self.o, radix, stride) * self.sub
        own = self.rows_at(base, self.sub)
        total = self.part[own]
        for k in range(radix - 1):
            total = total + self.recv[pl.ds(self.used + k * self.sub, self.sub)]
        if target is None:
            self.part[own] = total
        else:
            target[own] = total
        self.used += (radix - 1) * self.sub
        self.base, self.size = base, self.sub

    def gather_start(self, stage):
        radix, stride = self.plan[stage]
        self.flight = []
        for k in range(radix - 1):
            to, digit, other = peer_of(self.o, radix, stride, k)
            here = self.full.at[self.rows_at(self.base, self.size)]
            copy = pltpu.make_async_remote_copy(
                src_ref=here,
                dst_ref=here,
                send_sem=self.gather_send.at[stage, k],
                recv_sem=self.gather_recv.at[stage, k],
                device_id=(self.r, to),
                device_id_type=MESH,
            )
            copy.start()
            self.flight.append(copy)

    def gather_finish(self, stage):
        radix, stride = self.plan[stage]
        for copy in self.flight:
            copy.wait()
        self.base = self.base - digit_of(self.o, radix, stride) * self.size
        self.size = self.size * radix


def sem_shape(plan):
    return (max(len(plan), 1), max([radix - 1 for radix, _ in plan] + [1]))


def section_sems(plan):
    return [pltpu.SemaphoreType.DMA(sem_shape(plan))] * 4


def split3(value):
    high = value.astype(BF16).astype(F32)
    rest = value - high
    middle = rest.astype(BF16).astype(F32)
    return high, middle, rest - middle


def cholesky_small(entries):
    order = len(entries)
    factor = [[None] * order for i in range(order)]
    for j in range(order):
        diagonal = entries[j][j]
        for k in range(j):
            diagonal = diagonal - factor[j][k] * factor[j][k]
        inverse = 1.0 / jnp.sqrt(diagonal)
        factor[j][j] = inverse
        for i in range(j + 1, order):
            current = entries[i][j]
            for k in range(j):
                current = current - factor[i][k] * factor[j][k]
            factor[i][j] = current * inverse
    return factor


def forward_small(factor, target):
    result = []
    for a in range(len(target)):
        current = target[a]
        for k in range(a):
            current = current - factor[a][k] * result[k]
        result.append(current * factor[a][a])
    return result


def backward_small(factor, target):
    order = len(target)
    result = [None] * order
    for a in reversed(range(order)):
        current = target[a]
        for k in range(a + 1, order):
            current = current - factor[k][a] * result[k]
        result[a] = current * factor[a][a]
    return result


def three_rows(row, width):
    sub = lax.broadcasted_iota(jnp.int32, (GROUP, width), 0)
    high, middle, low = (jnp.broadcast_to(piece, (GROUP, width)) for piece in split3(row))
    zero = jnp.zeros((GROUP, width), F32)
    return jnp.where(sub == 0, high, jnp.where(sub == 1, middle, jnp.where(sub == 2, low, zero))).astype(BF16)


def local_pieces(rows_ref, count_ref, prior_ref, observed, nparams):
    width = rows_ref.shape[1]
    objects = count_ref.shape[0]
    shape = (objects, width)
    lane = lax.broadcasted_iota(jnp.int32, shape, 1)
    sub = lax.broadcasted_iota(jnp.int32, shape, 0)
    counts = jnp.zeros(shape, jnp.int32)
    for n in range(objects):
        counts = jnp.where(sub == n, count_ref[n], counts)
    position = lane - sub * observed
    present = (position >= 0) & (position < counts)
    weights = jnp.where(present, jnp.broadcast_to(rows_ref[nparams + 1 : nparams + 2, :], shape), F32(0.0))
    counted = jnp.sum(jnp.where(present, F32(1.0), F32(0.0)))
    residual = rows_ref[nparams : nparams + 1, :]
    weight = jnp.sum(weights, axis=0, keepdims=True)
    misfit = jnp.sum(weight * residual * residual)
    weighted = jnp.concatenate(
        [jnp.broadcast_to(rows_ref[a : a + 1, :], shape) * weights for a in range(nparams)], axis=0
    )
    small = dot_nt(weighted, rows_ref[0 : nparams + 1, :])
    vreg = (objects, PANEL)
    row = lax.broadcasted_iota(jnp.int32, vreg, 0)

    def entry(a, b):
        return jnp.broadcast_to(small[a * objects : (a + 1) * objects, b : b + 1], vreg)

    def prior(a):
        value = jnp.zeros(vreg, F32)
        for n in range(objects):
            value = jnp.where(row == n, prior_ref[a, n], value)
        return value

    entries = [
        [entry(a, b) + prior(a) if a == b else (entry(a, b) if a > b else None) for b in range(nparams)]
        for a in range(nparams)
    ]
    factor = cholesky_small(entries)
    vector = forward_small(factor, [entry(a, nparams) for a in range(nparams)])
    return weights, weight, residual, misfit, counted, weighted, factor, vector


def normal_kernel(
    plan,
    n_regime,
    observed,
    nparams,
    regional_width,
    count_ref,
    prior_ref,
    rows_ref,
    index_ref,
    global_ref,
    rr_out,
    rg_out,
    gg_out,
    reg_ref,
    weighted_ref,
    factor_ref,
    scaled_r,
    scaled_g,
    reduced,
    scalars,
    rr_part,
    rr_recv,
    rr_full,
    rg_part,
    rg_recv,
    rg_full,
    gg_part,
    gg_recv,
    scalar_send,
    scalar_recv,
    *sems,
):
    barrier, total = enter(plan, n_regime)
    r, o = lax.axis_index("regime"), lax.axis_index("obj")
    width = rows_ref.shape[1]
    global_width = global_ref.shape[1]
    objects = count_ref.shape[0]
    columns = regional_width + global_width
    rt, gt = regional_width // PANEL, global_width // PANEL
    rr_tiles = {tile: at for at, tile in enumerate(tiles_upper(rt))}
    gg_tiles = {tile: at for at, tile in enumerate(tiles_upper(gt))}

    weights, weight, residual, misfit, counted, weighted, factor, vector = local_pieces(
        rows_ref, count_ref, prior_ref, observed, nparams
    )
    tile = (GROUP, PANEL)
    sub = lax.broadcasted_iota(jnp.int32, tile, 0)
    scalars[0] = jnp.where(sub == 0, misfit, jnp.where(sub == 1, counted, F32(0.0)))
    pl.semaphore_wait(barrier, total)
    shared = []
    for k in range(n_regime - 1):
        copy = pltpu.make_async_remote_copy(
            src_ref=scalars.at[0],
            dst_ref=scalars.at[k + 1],
            send_sem=scalar_send.at[k],
            recv_sem=scalar_recv.at[k],
            device_id=(lax.rem(r + k + 1, n_regime), o),
            device_id_type=MESH,
        )
        copy.start()
        shared.append(copy)

    weighted_ref[...] = weighted
    at = 0
    for a in range(nparams):
        for b in range(a + 1):
            factor_ref[at * objects : (at + 1) * objects, :] = factor[a][b]
            at += 1

    shape = (regional_width, width)
    ids = lax.broadcasted_iota(jnp.int32, shape, 0)
    regional = jnp.zeros(shape, F32)
    taps = index_ref.shape[0]
    for k in range(taps):
        at = nparams + 2 + k
        regional = regional + jnp.where(
            jnp.broadcast_to(index_ref[k : k + 1, :], shape) == ids,
            jnp.broadcast_to(rows_ref[at : at + 1, :], shape),
            F32(0.0),
        )
    regional = regional.astype(BF16)
    reg_ref[...] = regional
    scaled_r[...] = (regional.astype(F32) * weight).astype(BF16)
    wide = -(-width // PANEL) * PANEL
    eight = jnp.broadcast_to(weight, (GROUP, width))
    if wide > width:
        eight = jnp.concatenate([eight, jnp.zeros((GROUP, wide - width), F32)], axis=1)
    column = jnp.transpose(eight)[:width, 0:1]
    scaled_g[...] = (global_ref[...].astype(F32) * column).astype(BF16)

    three = jnp.concatenate(split3(weighted), axis=0).astype(BF16)
    held = nparams * objects
    reg3 = dot_nt(three, reg_ref[...], None)
    glo3 = dot_nn(three, global_ref[...], None)
    coupling = [
        piece[0:held] + piece[held : 2 * held] + piece[2 * held : 3 * held] for piece in (reg3, glo3)
    ]
    res3 = three_rows(residual, width)
    gradient = [
        jnp.sum(dot_nt(res3, scaled_r[...], None), axis=0, keepdims=True),
        jnp.sum(dot_nn(res3, scaled_g[...], None), axis=0, keepdims=True),
    ]
    extra = len(rr_tiles) * PANEL
    for c in range(columns // PANEL):
        side, at = (0, c * PANEL) if c < rt else (1, c * PANEL - regional_width)
        cols = slice(at, at + PANEL)
        result = forward_small(
            factor, [coupling[side][a * objects : (a + 1) * objects, cols] for a in range(nparams)]
        )
        dropped = vector[0] * result[0]
        for a in range(1, nparams):
            dropped = dropped + vector[a] * result[a]
        for a in range(nparams):
            reduced[a * objects : (a + 1) * objects, c * PANEL : (c + 1) * PANEL] = result[a]
        rr_part[extra + c : extra + c + 1, :] = gradient[side][:, cols] - jnp.sum(dropped, axis=0, keepdims=True)
    for copy in shared:
        copy.wait()
    both = scalars[0]
    for k in range(n_regime - 1):
        both = both + scalars[k + 1]
    at = extra + columns // PANEL
    rr_part[at : at + GROUP, :] = both
    if at + GROUP < rr_part.shape[0]:
        rr_part[at + GROUP :, :] = jnp.zeros((rr_part.shape[0] - at - GROUP, PANEL), F32)

    first, second, third = split3(reduced[...])
    left = jnp.concatenate([first, first, second, first, second, third], axis=0).astype(BF16)
    right = jnp.concatenate([first, second, first, third, second, first], axis=0).astype(BF16)

    rr = Section(rr_part.shape[0], plan, rr_part, rr_recv, rr_full, sems[0:4])
    rg = Section(rg_part.shape[0], plan, rg_part, rg_recv, rg_full, sems[4:8])
    gg = Section(gg_part.shape[0], plan, gg_part, gg_recv, None, sems[8:12])

    for i in range(rt):
        own, rest = slice(i * PANEL, (i + 1) * PANEL), slice(i * PANEL, regional_width)
        line = dot_nt(scaled_r[own, :], reg_ref[rest, :], None) + dot_nt(reg_ref[own, :], scaled_r[rest, :], None)
        line = 0.5 * line - dot_tn(left[:, own], right[:, rest], None)
        for j in range(i, rt):
            at = rr_tiles[i, j] * PANEL
            rr_part[at : at + PANEL, :] = line[:, (j - i) * PANEL : (j - i + 1) * PANEL]
    if plan:
        rr.scatter_start(0)
    for i in range(rt):
        own = slice(i * PANEL, (i + 1) * PANEL)
        line = dot_nn(scaled_r[own, :], global_ref[...], None)
        line = line - dot_tn(left[:, own], right[:, regional_width:], None)
        for j in range(gt):
            at = (i * gt + j) * PANEL
            rg_part[at : at + PANEL, :] = line[:, j * PANEL : (j + 1) * PANEL]
    for at in range(rt * gt * PANEL, rg_part.shape[0], GROUP):
        rg_part[at : at + GROUP, :] = jnp.zeros(tile, F32)
    if plan:
        rg.scatter_start(0)
        rr.scatter_finish(0)
        if len(plan) > 1:
            rr.scatter_start(1)
    for i in range(gt):
        own, rest = slice(i * PANEL, (i + 1) * PANEL), slice(i * PANEL, global_width)
        line = dot_tn(scaled_g[:, own], global_ref[:, rest], None) + dot_tn(global_ref[:, own], scaled_g[:, rest], None)
        shift = regional_width
        line = 0.5 * line - dot_tn(
            left[:, shift + i * PANEL : shift + (i + 1) * PANEL], right[:, shift + i * PANEL :], None
        )
        for j in range(i, gt):
            at = gg_tiles[i, j] * PANEL
            gg_part[at : at + PANEL, :] = line[:, (j - i) * PANEL : (j - i + 1) * PANEL]
    for at in range(len(gg_tiles) * PANEL, gg_part.shape[0], GROUP):
        gg_part[at : at + GROUP, :] = jnp.zeros(tile, F32)
    last = len(plan) - 1
    if plan:
        gg.scatter_start(0)
        for stage in range(len(plan)):
            for section in (rg, gg):
                section.scatter_finish(stage, rg_full if stage == last and section is rg else None)
                if stage < last:
                    section.scatter_start(stage + 1)
            if stage > 0:
                rr.scatter_finish(stage, rr_full if stage == last else None)
                if stage < last:
                    rr.scatter_start(stage + 1)
        for stage in reversed(range(len(plan))):
            for section in (rr, rg):
                section.gather_start(stage)
            for section in (rr, rg):
                section.gather_finish(stage)
    rr_out[...] = rr_full[...] if plan else rr_part[...]
    rg_out[...] = rg_full[...] if plan else rg_part[...]
    own = owned_base(o, gg_part.shape[0], plan)
    gg_out[...] = gg_part[pl.ds(pl.multiple_of(own, GROUP) if plan else 0, gg_out.shape[0]), :]


def inverse_factor(block):
    order = block.shape[0]
    lane = lax.broadcasted_iota(jnp.int32, (GROUP, order), 1)
    sub = lax.broadcasted_iota(jnp.int32, (GROUP, order), 0)
    shape = (GROUP, order)
    chunks = [block[i * GROUP : (i + 1) * GROUP, :] for i in range(order // GROUP)]
    for g in range(order // GROUP):
        base = g * GROUP
        inside = (lane >= base) & (lane < base + GROUP)
        cols = {
            i: [jnp.broadcast_to(chunks[i][:, base + b : base + b + 1], shape) for b in range(GROUP)]
            for i in range(g, len(chunks))
        }
        small = [
            [jnp.broadcast_to(cols[g][b][a : a + 1, :], shape) if a >= b else None for b in range(GROUP)]
            for a in range(GROUP)
        ]
        rows = [
            jnp.where(
                lane == base + b,
                jnp.float32(1.0),
                jnp.where(inside, jnp.float32(0.0), jnp.broadcast_to(chunks[g][b : b + 1, :], shape)),
            )
            for b in range(GROUP)
        ]
        inverse = []
        for b in range(GROUP):
            recip = 1.0 / small[b][b]
            inverse.append(recip)
            ratio = [small[a][b] * recip if a > b else None for a in range(GROUP)]
            for a in range(b + 1, GROUP):
                rows[a] = rows[a] - ratio[a] * rows[b]
                for c in range(b + 1, a + 1):
                    small[a][c] = small[a][c] - ratio[a] * small[c][b]
            for i in range(g + 1, len(chunks)):
                for c in range(b + 1, GROUP):
                    cols[i][c] = cols[i][c] - cols[i][b] * ratio[c]
        scaled_rows = [rows[b] * inverse[b] for b in range(GROUP)]
        for i in range(g + 1, len(chunks)):
            current = jnp.where(inside, jnp.float32(0.0), chunks[i])
            for b in range(GROUP):
                current = current - cols[i][b] * scaled_rows[b]
            chunks[i] = current
        final = jnp.zeros(shape, jnp.float32)
        for b in range(GROUP):
            final = jnp.where(sub == b, rows[b] / jnp.sqrt(small[b][b]), final)
        chunks[g] = jnp.where(lane <= sub + base, final, jnp.float32(0.0))
    return jnp.concatenate(chunks, axis=0)


def eliminate(work, inv, y):
    order = work.shape[0]
    count = order // PANEL

    def panel(p, carry):
        for q in range(1, count):
            @pl.when(p == q)
            def update(q=q):
                at = q * PANEL
                above = work[0:at, at : at + PANEL]
                work[at : at + PANEL, at:] = work[at : at + PANEL, at:] - dot_tn(above, work[0:at, at:])
                y[:, at : at + PANEL] = y[:, at : at + PANEL] - dot_nn(y[:, 0:at], above)

        at = pl.multiple_of(p * PANEL, PANEL)
        inv[pl.ds(at, PANEL), :] = inverse_factor(work[pl.ds(at, PANEL), pl.ds(at, PANEL)])
        for q in range(count):
            @pl.when(p == q)
            def apply(q=q):
                at = q * PANEL
                own = inv[at : at + PANEL, :]
                if at + PANEL < work.shape[1]:
                    work[at : at + PANEL, at + PANEL :] = dot_nn(own, work[at : at + PANEL, at + PANEL :])
                y[:, at : at + PANEL] = dot_nt(y[:, at : at + PANEL], own)

        return carry

    lax.fori_loop(0, count, panel, 0)


def back_substitute(work, inv, y):
    order = work.shape[0]
    for q in reversed(range(order // PANEL)):
        at = q * PANEL
        current = y[:, at : at + PANEL]
        if at + PANEL < order:
            current = current - dot_nt(y[:, at + PANEL : order], work[at : at + PANEL, at + PANEL : order])
        y[:, at : at + PANEL] = dot_nn(current, inv[at : at + PANEL, :])


def add_diagonal(work, prior, damping):
    order = work.shape[0]
    rows = lax.broadcasted_iota(jnp.int32, (PANEL, PANEL), 0)
    columns = lax.broadcasted_iota(jnp.int32, (PANEL, PANEL), 1)
    for q in range(order // PANEL):
        at = q * PANEL
        extra = jnp.broadcast_to(prior[0:1, at : at + PANEL] * damping, (PANEL, PANEL))
        tile = work[at : at + PANEL, at : at + PANEL]
        work[at : at + PANEL, at : at + PANEL] = tile + jnp.where(rows == columns, extra, F32(0.0))


def regional_kernel(gt, rr, rg, prior, work, inv, y, gram, vec, damp):
    width = work.shape[0]
    rt = width // PANEL
    for at, (i, j) in enumerate(tiles_upper(rt)):
        work[i * PANEL : (i + 1) * PANEL, j * PANEL : (j + 1) * PANEL] = rr[at * PANEL : (at + 1) * PANEL, :]
    for i in range(rt):
        for j in range(gt):
            at = (i * gt + j) * PANEL
            work[i * PANEL : (i + 1) * PANEL, width + j * PANEL : width + (j + 1) * PANEL] = rg[at : at + PANEL, :]
    extra = len(tiles_upper(rt)) * PANEL
    for c in range(rt):
        y[:, c * PANEL : (c + 1) * PANEL] = jnp.broadcast_to(rr[extra + c : extra + c + 1, :], (GROUP, PANEL))
    at = extra + rt + gt
    damping = rr[at : at + 1, :] / rr[at + 1 : at + 2, :]
    damp[...] = jnp.broadcast_to(damping, damp.shape)
    add_diagonal(work, prior, damping)
    eliminate(work, inv, y)
    for i in range(gt):
        line = dot_tn(work[:, width + i * PANEL : width + (i + 1) * PANEL], work[:, width + i * PANEL :])
        for j in range(i, gt):
            at = tiles_upper(gt).index((i, j)) * PANEL
            gram[at : at + PANEL, :] = line[:, (j - i) * PANEL : (j - i + 1) * PANEL]
    if gram.shape[0] > len(tiles_upper(gt)) * PANEL:
        at = len(tiles_upper(gt)) * PANEL
        gram[at:, :] = jnp.zeros((gram.shape[0] - at, PANEL), F32)
    dropped = dot_nn(y[...], work[:, width:])
    for j in range(gt):
        at = extra + rt + j
        vec[j : j + 1, :] = rr[at : at + 1, :] - dropped[0:1, j * PANEL : (j + 1) * PANEL]
    if gt < GROUP:
        vec[gt:, :] = jnp.zeros((GROUP - gt, PANEL), F32)


def join_kernel(
    plan,
    n_regime,
    gram,
    own_ref,
    vec,
    total_out,
    vec_out,
    part,
    part_recv,
    vec_part,
    full,
    share_send,
    share_recv,
    *sems,
):
    barrier, total = enter(plan, n_regime)
    r, o = lax.axis_index("regime"), lax.axis_index("obj")
    size = own_ref.shape[0]
    base = owned_base(o, gram.shape[0], plan)
    base = pl.multiple_of(base, GROUP) if plan else 0
    part[...] = own_ref[...] - gram[pl.ds(base, size), :]
    vec_part[0] = vec[...]
    pl.semaphore_wait(barrier, total)
    copies = []
    for k in range(n_regime - 1):
        to = (lax.rem(r + k + 1, n_regime), o)
        for which, (src, dst) in enumerate(
            ((part, part_recv.at[k]), (vec_part.at[0], vec_part.at[k + 1]))
        ):
            copy = pltpu.make_async_remote_copy(
                src_ref=src,
                dst_ref=dst,
                send_sem=share_send.at[k, which],
                recv_sem=share_recv.at[k, which],
                device_id=to,
                device_id_type=MESH,
            )
            copy.start()
            copies.append(copy)
    for copy in copies:
        copy.wait()
    value, vector = None, None
    for g in range(n_regime):
        piece, line = part[...], vec_part[0]
        for k in range(n_regime - 1):
            chosen = lax.rem(r + n_regime - k - 1, n_regime) == g
            piece = jnp.where(chosen, part_recv[k], piece)
            line = jnp.where(chosen, vec_part[k + 1], line)
        value = piece if value is None else value + piece
        vector = line if vector is None else vector + line
    full[pl.ds(base, size), :] = value
    vec_out[...] = vector
    section = Section(full.shape[0], plan, None, None, full, (None, None) + sems)
    section.base, section.size = base, size
    for stage in reversed(range(len(plan))):
        section.gather_start(stage)
        section.gather_finish(stage)
    total_out[...] = full[...]


def final_kernel(
    nparams,
    matrix,
    vec,
    gprior,
    damp,
    work,
    inv,
    y,
    rows_ref,
    global_ref,
    reg_ref,
    weighted_ref,
    factor_ref,
    local_step,
    regional_step,
    global_step,
    gwork,
    ginv,
    gy,
    ry,
):
    width = work.shape[0]
    order = gwork.shape[0]
    gt = order // PANEL
    for at, (i, j) in enumerate(tiles_upper(gt)):
        gwork[i * PANEL : (i + 1) * PANEL, j * PANEL : (j + 1) * PANEL] = matrix[at * PANEL : (at + 1) * PANEL, :]
    add_diagonal(gwork, gprior, damp[0:1, :])
    for j in range(gt):
        gy[:, j * PANEL : (j + 1) * PANEL] = jnp.broadcast_to(vec[j : j + 1, :], (GROUP, PANEL))
    eliminate(gwork, ginv, gy)
    back_substitute(gwork, ginv, gy)
    global_step[...] = gy[0:1, :]
    ry[...] = y[...] - dot_nt(gy[...], work[:, width:])
    back_substitute(work, inv, ry)
    regional_step[...] = ry[0:1, :]
    moved = dot_nn(three_rows(ry[0:1, :], width), reg_ref[...], None)
    moved = moved + dot_nt(three_rows(gy[0:1, :], order), global_ref[...], None)
    moved = jnp.sum(moved, axis=0, keepdims=True)
    left = rows_ref[nparams : nparams + 1, :] - moved
    target = jnp.sum(weighted_ref[...] * left, axis=1, keepdims=True)
    objects = weighted_ref.shape[0] // nparams
    vreg = (objects, PANEL)
    targets = [jnp.broadcast_to(target[a * objects : (a + 1) * objects, :], vreg) for a in range(nparams)]
    factor, at = [], 0
    for a in range(nparams):
        line = []
        for b in range(a + 1):
            line.append(factor_ref[at * objects : (at + 1) * objects, :])
            at += 1
        factor.append(line)
    solved = backward_small(factor, forward_small(factor, targets))
    lane = lax.broadcasted_iota(jnp.int32, vreg, 1)
    joined = jnp.zeros(vreg, F32)
    for a in range(nparams):
        joined = jnp.where(lane == a, solved[a], joined)
    local_step[...] = jnp.transpose(joined)[0:nparams, 0:objects]


def vmem(count):
    return [pl.BlockSpec(memory_space=pltpu.VMEM)] * count


def smem(count):
    return [pl.BlockSpec(memory_space=pltpu.SMEM)] * count


def shaped(*shape, dtype=F32):
    return jax.ShapeDtypeStruct(shape, dtype)


def body(
    n_regime,
    n_obj,
    local_jac,
    global_jac,
    coeff_index,
    coeff_weight,
    residual,
    obs_weight,
    obs_count,
    local_prior,
    regional_prior,
    global_prior,
):
    nparams, width = local_jac.shape
    objects = obs_count.shape[0]
    observed = width // objects
    regional_width, order = regional_prior.shape[1], global_jac.shape[1]
    rt, gt = regional_width // PANEL, order // PANEL
    plan = stage_plan(n_obj)
    taps = coeff_index.shape[0]
    rows = jnp.concatenate(
        [local_jac.astype(F32), residual[None, :], obs_weight[None, :], coeff_weight.astype(F32)], axis=0
    )
    rr_rows = padded(len(tiles_upper(rt)) * PANEL + rt + gt + GROUP, n_obj)
    rg_rows = padded(rt * gt * PANEL, n_obj)
    gg_rows = padded(len(tiles_upper(gt)) * PANEL, n_obj)
    own = gg_rows // n_obj
    held = nparams * objects
    entries = nparams * (nparams + 1) // 2
    columns = regional_width + order
    peers = max(n_regime - 1, 1)

    def buffer(*shape, dtype=F32):
        return pltpu.VMEM(shape, dtype)

    rr, rg, gg, reg, weighted, factor = pl.pallas_call(
        functools.partial(normal_kernel, plan, n_regime, observed, nparams, regional_width),
        out_shape=(
            shaped(rr_rows, PANEL),
            shaped(rg_rows, PANEL),
            shaped(own, PANEL),
            shaped(regional_width, width, dtype=BF16),
            shaped(held, width),
            shaped(entries * objects, PANEL),
        ),
        in_specs=smem(2) + vmem(3),
        out_specs=tuple(vmem(6)),
        scratch_shapes=[
            buffer(regional_width, width, dtype=BF16),
            buffer(width, order, dtype=BF16),
            buffer(held, columns),
            buffer(n_regime, GROUP, PANEL),
            buffer(rr_rows, PANEL),
            buffer(rr_rows, PANEL),
            buffer(rr_rows, PANEL),
            buffer(rg_rows, PANEL),
            buffer(rg_rows, PANEL),
            buffer(rg_rows, PANEL),
            buffer(gg_rows, PANEL),
            buffer(gg_rows, PANEL),
            pltpu.SemaphoreType.DMA((peers,)),
            pltpu.SemaphoreType.DMA((peers,)),
        ]
        + section_sems(plan) * 3,
        compiler_params=pltpu.CompilerParams(collective_id=0, has_side_effects=True),
        name="normal",
    )(obs_count, local_prior, rows, coeff_index, global_jac)

    work, inv, y, gram, vec, damp = pl.pallas_call(
        functools.partial(regional_kernel, gt),
        out_shape=(
            shaped(regional_width, columns),
            shaped(regional_width, PANEL),
            shaped(GROUP, regional_width),
            shaped(gg_rows, PANEL),
            shaped(GROUP, PANEL),
            shaped(GROUP, PANEL),
        ),
        in_specs=vmem(3),
        out_specs=tuple(vmem(6)),
        name="regional",
    )(rr, rg, regional_prior)

    matrix, vec = pl.pallas_call(
        functools.partial(join_kernel, plan, n_regime),
        out_shape=(shaped(gg_rows, PANEL), shaped(GROUP, PANEL)),
        in_specs=vmem(3),
        out_specs=tuple(vmem(2)),
        scratch_shapes=[
            buffer(own, PANEL),
            buffer(peers, own, PANEL),
            buffer(n_regime, GROUP, PANEL),
            buffer(gg_rows, PANEL),
            pltpu.SemaphoreType.DMA((peers, 2)),
            pltpu.SemaphoreType.DMA((peers, 2)),
        ]
        + section_sems(plan)[:2],
        compiler_params=pltpu.CompilerParams(collective_id=1, has_side_effects=True),
        name="join",
    )(gram, gg, vec)

    local_step, regional_step, global_step = pl.pallas_call(
        functools.partial(final_kernel, nparams),
        out_shape=(shaped(nparams, objects), shaped(1, regional_width), shaped(1, order)),
        in_specs=vmem(12),
        out_specs=tuple(vmem(3)),
        scratch_shapes=[
            buffer(order, order),
            buffer(order, PANEL),
            buffer(GROUP, order),
            buffer(GROUP, regional_width),
        ],
        name="final",
    )(matrix, vec, global_prior[None, :], damp, work, inv, y, rows, global_jac, reg, weighted, factor)
    return (local_step, regional_step, global_step[0])


def solution(mesh):
    return jax.shard_map(
        functools.partial(body, mesh.shape["regime"], mesh.shape["obj"]),
        mesh=mesh,
        in_specs=(
            P(None, ("regime", "obj")),
            P(("regime", "obj"), None),
            P(None, ("regime", "obj")),
            P(None, ("regime", "obj")),
            P(("regime", "obj")),
            P(("regime", "obj")),
            P(("regime", "obj")),
            P(None, ("regime", "obj")),
            P("regime", None),
            P(),
        ),
        out_specs=(P(None, ("regime", "obj")), P("regime", None), P()),
        check_vma=False,
    )
```

time: 353 us -> 140 us (0.40)
  waiting for transfers between devices: 190 us -> 0 us
  Pallas kernels: 55.3 us -> 137 us
  blocking collectives: 42.6 us -> 0 us
  local copies, waits for them, and re-layouts: 22.6 us -> 0 us
  other arithmetic: 19.1 us -> 2.72 us
  between operations: 15.4 us -> 0.65 us
  matrix products: 7.32 us -> 0 us
    psum x3 -> x0, waiting for transfers between devices: 190 us -> none  [the longest x1 95.3 us: body(): global_block = lax.psum(schur[width:, width:], ('regime', 'obj'))]
    pallas_call x2 -> x4, Pallas kernels: 55.3 us -> 137 us  [the longest x1 59.2 us: body(): pl.pallas_call(functools.partial(normal_kernel, plan, n_regime, observed,...]
    psum x1 -> x0, blocking collectives: 42.6 us -> none  [body(): lax.psum((jnp.sum(weight * residual * residual), jnp.sum(present.astype(j...]
    slice x17 -> x0, local copies, waits for them, and re-layouts: 13.5 us -> none  [the longest x3 5.55 us: body(): regional_block, block = (upper[:width, :width], upper[:width, width:])]
    dot_general x7 -> x0, matrix products: 7.32 us -> none  [the longest x1 3.52 us: body(): jnp.dot(stacked.T, stacked, precision=lax.Precision.HIGHEST)]
    concatenate x5 -> x1, other arithmetic: 5.87 us -> 1.33 us  [body(): jnp.concatenate([local_jac.astype(F32), residual[None, :], obs_weight[Non...]
    add x2 -> x0, other arithmetic: 3.86 us -> none  [the longest x1 2.43 us: body(): global_block + reduced_global[:-1]]
  transfers between devices with their start and end apart: 3 -> 0, of which waited for: 3 -> 0; matrix products, arithmetic and copies ran while one was open for 6% -> 0% of each run, Pallas kernels for 8% -> 0%
where the time goes in v1:
time: 140 us
  Pallas kernels  137 us (98%)
  other arithmetic  2.72 us (2%)
    pallas_call x1, Pallas kernels, body(): pl.pallas_call(functools.partial(normal_kernel, plan, n_regime, observed,...  59.2 us
    pallas_call x1, Pallas kernels, body(): pl.pallas_call(functools.partial(final_kernel, nparams), out_shape=(shape...  29.1 us
    pallas_call x1, Pallas kernels, body(): pl.pallas_call(functools.partial(regional_kernel, gt), out_shape=(shaped(...  26.9 us
    pallas_call x1, Pallas kernels, body(): pl.pallas_call(functools.partial(join_kernel, plan, n_regime), out_shape=...  21.5 us

profile of v1, /device:TPU:0, one launch (start us, length us, event | category | flops | bytes accessed | tf_op | source)
XLA Modules:
  0.0 140.1 jit_solution(477150010497617030)
XLA Ops:
  0.6 0.7 convert_element_type.7
  1.3 0.7 convert_element_type.6
  2.0 1.3 pad_maximum_fusion.rows_ref
  3.3 59.2 %normal.1 = (f32[1408,128]{1,0:T(8,128)}, f32[2048,128]{1,0:T(8,128)}, f32[80,128]{1,0:T(8,128)}, bf16[512,480]{1,0:T(8,128)(2,1)}, f32[56,480]{1,0:T(8,128)}, /*index=5*/f32[224,128]{1,0:T(8,128)}) custom-call(s32[8]{0:T(128)} %count_ref.1, f32[7,8]{1,0:T(8,128)} %prior_ref.1, f32[13,480]{1,0:T(8,128)} %pad_maximum_fusion.rows_ref, s32[4,480]{1,0:T(4,128)} %index_ref.1, ...), custom_call_target="tpu_custom_call" | custom-call | tf_op jit(solution)/shard_map/normal/pallas_call | solution.py:756
  62.6 26.9 %regional.1 = (f32[512,1024]{1,0:T(8,128)}, f32[512,128]{1,0:T(8,128)}, f32[8,512]{1,0:T(8,128)}, f32[1280,128]{1,0:T(8,128)}, f32[8,128]{1,0:T(8,128)}, /*index=5*/f32[8,128]{1,0:T(8,128)}) custom-call(f32[1408,128]{1,0:T(8,128)} %get-tuple-element.20.rr, f32[2048,128]{1,0:T(8,128)} %get-tuple-element.21.rg, f32[1,512]{1,0:T(1,128)} %prior.1), custom_call_target="tpu_custom_call" | custom-call | tf_op jit(solution)/shard_map/regional/pallas_call | solution.py:789
  89.4 21.5 %join.1 = (f32[1280,128]{1,0:T(8,128)}, f32[8,128]{1,0:T(8,128)}) custom-call(f32[1280,128]{1,0:T(8,128)} %get-tuple-element.22.gram, f32[80,128]{1,0:T(8,128)} %get-tuple-element.23.own_ref, f32[8,128]{1,0:T(8,128)} %get-tuple-element.24.vec), custom_call_target="tpu_custom_call" | custom-call | tf_op jit(solution)/shard_map/join/pallas_call | solution.py:804
  111.0 29.1 %final.1 = (f32[7,8]{1,0:T(8,128)}, f32[1,512]{1,0:T(1,128)}, f32[1,512]{1,0:T(1,128)}) custom-call(f32[1280,128]{1,0:T(8,128)} %get-tuple-element.25.matrix, f32[8,128]{1,0:T(8,128)} %get-tuple-element.26.vec, f32[1,512]{1,0:T(1,128)} %bitcast.4, f32[8,128]{1,0:T(8,128)} %get-tuple-element.27.damp, f32[512,1024]{1,0:T(8,128)} %get-tuple-element.28.work, ...), custom_call_target="tpu_custom_call" | custom-call | tf_op jit(solution)/shard_map/final/pallas_call | solution.py:822

commit v2 on v0

v2 whole, which is shorter than its diff:
```python
import functools

import jax
import jax.numpy as jnp
from jax import lax
from jax.experimental import pallas as pl
from jax.experimental.pallas import tpu as pltpu
from jax.sharding import PartitionSpec as P

PANEL = 128
GROUP = 8
FULL = lax.Precision.HIGHEST
F32 = jnp.float32
BF16 = jnp.bfloat16
MESH = pl.DeviceIdType.MESH


def dot(left, right, contract, precision=None):
    return lax.dot_general(
        left, right, ((contract[:1], contract[1:]), ((), ())), precision=precision, preferred_element_type=F32
    )


def dot_tn(left, right, precision=FULL):
    return dot(left, right, (0, 0), precision)


def dot_nt(left, right, precision=FULL):
    return dot(left, right, (1, 1), precision)


def dot_nn(left, right, precision=FULL):
    return dot(left, right, (1, 0), precision)


def tiles_upper(count):
    return [(i, j) for i in range(count) for j in range(i, count)]


def stage_plan(count):
    plan, stride = [], 1
    while stride < count:
        left = count // stride
        if stride < 4 and left % 2 == 0:
            radix = 2
        elif left % 4 == 0:
            radix = 4
        else:
            radix = left
        plan.append((radix, stride))
        stride *= radix
    return tuple(plan)


def padded(rows, count):
    unit = GROUP * count
    return -(-rows // unit) * unit


def digit_of(o, radix, stride):
    return lax.rem(lax.div(o, stride), radix)


def peer_of(o, radix, stride, k):
    digit = digit_of(o, radix, stride)
    other = lax.rem(digit + k + 1, radix)
    return o + (other - digit) * stride, digit, other


def owned_base(o, rows, plan):
    base, size = 0, rows
    for radix, stride in plan:
        size = size // radix
        base = base + digit_of(o, radix, stride) * size
    return base


def enter(plan, n_regime):
    r, o = lax.axis_index("regime"), lax.axis_index("obj")
    barrier = pltpu.get_barrier_semaphore()
    total = 0
    for radix, stride in plan:
        for k in range(radix - 1):
            pl.semaphore_signal(barrier, inc=1, device_id=(r, peer_of(o, radix, stride, k)[0]), device_id_type=MESH)
            total += 1
    for k in range(n_regime - 1):
        pl.semaphore_signal(barrier, inc=1, device_id=(lax.rem(r + k + 1, n_regime), o), device_id_type=MESH)
        total += 1
    return barrier, total


class Section:
    def __init__(self, plan, part, recv, full, sems):
        self.plan, self.part, self.recv, self.full, self.sems = plan, part, recv, full, sems
        r, o = lax.axis_index("regime"), lax.axis_index("obj")
        self.rows = part.shape[0]
        base, size, used = 0, self.rows, 0
        self.steps = []
        gathers = []
        for stage, (radix, stride) in enumerate(plan):
            sub = size // radix
            digit = digit_of(o, radix, stride)
            own = pl.multiple_of(base + digit * sub, GROUP)
            to, there = [], []
            for k in range(radix - 1):
                device, _, other = peer_of(o, radix, stride, k)
                to.append((r, device))
                there.append(pl.multiple_of(base + other * sub, GROUP))
            self.steps.append(("scatter", stage, to, there, own, sub, used))
            gathers.append(("gather", stage, to, None, own, sub, None))
            used += (radix - 1) * sub
            base, size = own, sub
        self.own, self.size = base, size
        self.steps += gathers[::-1]
        self.at = 0

    def copies(self, at):
        kind, stage, to, there, own, sub, used = self.steps[at]
        result = []
        for k, device in enumerate(to):
            if kind == "scatter":
                src = self.part.at[pl.ds(there[k], sub)]
                dst = self.recv.at[pl.ds(used + k * sub, sub)]
                send, recv = self.sems[0], self.sems[1]
            else:
                src = dst = self.full.at[pl.ds(own, sub)]
                send, recv = self.sems[2], self.sems[3]
            result.append(
                pltpu.make_async_remote_copy(
                    src_ref=src,
                    dst_ref=dst,
                    send_sem=send.at[stage, k],
                    recv_sem=recv.at[stage, k],
                    device_id=device,
                    device_id_type=MESH,
                )
            )
        return result

    def start(self):
        for copy in self.copies(self.at):
            copy.start()

    def finish(self):
        for copy in self.copies(self.at):
            copy.wait()
        kind, stage, to, there, own, sub, used = self.steps[self.at]
        if kind == "scatter":
            rows = pl.ds(own, sub)
            total = self.part[rows, :]
            for k in range(len(to)):
                total = total + self.recv[used + k * sub : used + (k + 1) * sub, :]
            target = self.full if stage == len(self.plan) - 1 else self.part
            target[rows, :] = total
        self.at += 1

    def next(self):
        self.finish()
        if self.at < len(self.steps):
            self.start()

    def rest(self):
        while self.at < len(self.steps):
            self.next()

    def result(self):
        return self.full if self.plan else self.part


class Join:
    def __init__(self, plan, n_regime, part, recv, full, sems):
        self.plan, self.part, self.recv, self.full, self.sems = plan, part, recv, full, sems
        self.n_regime = n_regime
        self.r, self.o = lax.axis_index("regime"), lax.axis_index("obj")
        self.radix, self.stride = plan[0] if plan else (1, 1)
        self.sub = part.shape[0] // self.radix
        digit = digit_of(self.o, self.radix, self.stride)
        self.own = pl.multiple_of(digit * self.sub, GROUP)
        self.across = [(lax.rem(self.r + k + 1, n_regime), self.o) for k in range(n_regime - 1)]
        self.beside = [(self.r, peer_of(self.o, self.radix, self.stride, k)[0]) for k in range(self.radix - 1)]
        self.mine = [lax.rem(self.r + n_regime - k - 1, n_regime) for k in range(n_regime - 1)]

    def copies(self, step):
        result = []
        rows = pl.ds(self.own, self.sub)
        for k, device in enumerate(self.across if step == 0 else self.beside):
            result.append(
                pltpu.make_async_remote_copy(
                    src_ref=(self.part if step == 0 else self.full).at[rows],
                    dst_ref=self.recv.at[k] if step == 0 else self.full.at[rows],
                    send_sem=self.sems[2 * step].at[k],
                    recv_sem=self.sems[2 * step + 1].at[k],
                    device_id=device,
                    device_id_type=MESH,
                )
            )
        return result

    def start(self):
        for copy in self.copies(0):
            copy.start()

    def add(self):
        for copy in self.copies(0):
            copy.wait()
        rows = pl.ds(self.own, self.sub)
        value = None
        for g in range(self.n_regime):
            piece = self.part[rows, :]
            for k in range(self.n_regime - 1):
                piece = jnp.where(self.mine[k] == g, self.recv[k], piece)
            value = piece if value is None else value + piece
        self.full[rows, :] = value
        for copy in self.copies(1):
            copy.start()

    def finish(self):
        for copy in self.copies(1):
            copy.wait()


def sem_shape(plan):
    return (max(len(plan), 1), max([radix - 1 for radix, _ in plan] + [1]))


def section_scratch(rows, plan):
    return [pltpu.VMEM((rows, PANEL), F32)] * 3 + [pltpu.SemaphoreType.DMA(sem_shape(plan))] * 4


def join_scratch(rows, plan, n_regime):
    radix = plan[0][0] if plan else 1
    return [
        pltpu.VMEM((rows, PANEL), F32),
        pltpu.VMEM((max(n_regime - 1, 1), rows // radix, PANEL), F32),
        pltpu.VMEM((rows, PANEL), F32),
        pltpu.SemaphoreType.DMA((max(n_regime - 1, 1),)),
        pltpu.SemaphoreType.DMA((max(n_regime - 1, 1),)),
        pltpu.SemaphoreType.DMA((max(radix - 1, 1),)),
        pltpu.SemaphoreType.DMA((max(radix - 1, 1),)),
    ]


def split3(value):
    high = value.astype(BF16).astype(F32)
    rest = value - high
    middle = rest.astype(BF16).astype(F32)
    return high, middle, rest - middle


def cholesky_small(entries):
    order = len(entries)
    factor = [[None] * order for i in range(order)]
    for j in range(order):
        diagonal = entries[j][j]
        for k in range(j):
            diagonal = diagonal - factor[j][k] * factor[j][k]
        inverse = 1.0 / jnp.sqrt(diagonal)
        factor[j][j] = inverse
        for i in range(j + 1, order):
            current = entries[i][j]
            for k in range(j):
                current = current - factor[i][k] * factor[j][k]
            factor[i][j] = current * inverse
    return factor


def forward_small(factor, target):
    result = []
    for a in range(len(target)):
        current = target[a]
        for k in range(a):
            current = current - factor[a][k] * result[k]
        result.append(current * factor[a][a])
    return result


def backward_small(factor, target):
    order = len(target)
    result = [None] * order
    for a in reversed(range(order)):
        current = target[a]
        for k in range(a + 1, order):
            current = current - factor[k][a] * result[k]
        result[a] = current * factor[a][a]
    return result


def three_rows(row, width):
    sub = lax.broadcasted_iota(jnp.int32, (GROUP, width), 0)
    high, middle, low = (jnp.broadcast_to(piece, (GROUP, width)) for piece in split3(row))
    zero = jnp.zeros((GROUP, width), F32)
    return jnp.where(sub == 0, high, jnp.where(sub == 1, middle, jnp.where(sub == 2, low, zero))).astype(BF16)


def local_pieces(local_ref, residual_ref, obs_ref, count_ref, prior_ref, rows8):
    nparams, width = local_ref.shape
    objects = count_ref.shape[0]
    observed = width // objects
    shape = (objects, width)
    lane = lax.broadcasted_iota(jnp.int32, shape, 1)
    sub = lax.broadcasted_iota(jnp.int32, shape, 0)
    counts = jnp.zeros(shape, jnp.int32)
    for n in range(objects):
        counts = jnp.where(sub == n, count_ref[n], counts)
    position = lane - sub * observed
    present = (position >= 0) & (position < counts)
    weights = jnp.where(present, jnp.broadcast_to(obs_ref[...], shape), F32(0.0))
    counted = jnp.sum(jnp.where(present, F32(1.0), F32(0.0)))
    residual = residual_ref[...]
    weight = jnp.sum(weights, axis=0, keepdims=True)
    misfit = jnp.sum(weight * residual * residual)
    rows8[0:nparams, :] = local_ref[...].astype(F32)
    rows8[nparams : nparams + 1, :] = residual
    weighted = jnp.concatenate(
        [jnp.broadcast_to(rows8[a : a + 1, :], shape) * weights for a in range(nparams)], axis=0
    )
    small = dot_nt(weighted, rows8[...])
    vreg = (objects, PANEL)
    row = lax.broadcasted_iota(jnp.int32, vreg, 0)

    def entry(a, b):
        return jnp.broadcast_to(small[a * objects : (a + 1) * objects, b : b + 1], vreg)

    def prior(a):
        value = jnp.zeros(vreg, F32)
        for n in range(objects):
            value = jnp.where(row == n, prior_ref[a, n], value)
        return value

    entries = [
        [entry(a, b) + prior(a) if a == b else (entry(a, b) if a > b else None) for b in range(nparams)]
        for a in range(nparams)
    ]
    factor = cholesky_small(entries)
    vector = forward_small(factor, [entry(a, nparams) for a in range(nparams)])
    return weight, residual, misfit, counted, weighted, factor, vector


def line_of_tiles(target, at, line):
    for j in range(line.shape[1] // PANEL):
        target[at : at + PANEL, :] = line[:, j * PANEL : (j + 1) * PANEL]
        at += PANEL
    return at


def clear(target, at):
    if at < target.shape[0]:
        target[at:, :] = jnp.zeros((target.shape[0] - at, PANEL), F32)


def inverse_factor(block):
    order = block.shape[0]
    lane = lax.broadcasted_iota(jnp.int32, (GROUP, order), 1)
    sub = lax.broadcasted_iota(jnp.int32, (GROUP, order), 0)
    shape = (GROUP, order)
    chunks = [block[i * GROUP : (i + 1) * GROUP, :] for i in range(order // GROUP)]
    for g in range(order // GROUP):
        base = g * GROUP
        inside = (lane >= base) & (lane < base + GROUP)
        cols = {
            i: [jnp.broadcast_to(chunks[i][:, base + b : base + b + 1], shape) for b in range(GROUP)]
            for i in range(g, len(chunks))
        }
        small = [
            [jnp.broadcast_to(cols[g][b][a : a + 1, :], shape) if a >= b else None for b in range(GROUP)]
            for a in range(GROUP)
        ]
        rows = [
            jnp.where(
                lane == base + b,
                jnp.float32(1.0),
                jnp.where(inside, jnp.float32(0.0), jnp.broadcast_to(chunks[g][b : b + 1, :], shape)),
            )
            for b in range(GROUP)
        ]
        inverse = []
        for b in range(GROUP):
            recip = 1.0 / small[b][b]
            inverse.append(recip)
            ratio = [small[a][b] * recip if a > b else None for a in range(GROUP)]
            for a in range(b + 1, GROUP):
                rows[a] = rows[a] - ratio[a] * rows[b]
                for c in range(b + 1, a + 1):
                    small[a][c] = small[a][c] - ratio[a] * small[c][b]
            for i in range(g + 1, len(chunks)):
                for c in range(b + 1, GROUP):
                    cols[i][c] = cols[i][c] - cols[i][b] * ratio[c]
        scaled_rows = [rows[b] * inverse[b] for b in range(GROUP)]
        for i in range(g + 1, len(chunks)):
            current = jnp.where(inside, jnp.float32(0.0), chunks[i])
            for b in range(GROUP):
                current = current - cols[i][b] * scaled_rows[b]
            chunks[i] = current
        final = jnp.zeros(shape, jnp.float32)
        for b in range(GROUP):
            final = jnp.where(sub == b, rows[b] / jnp.sqrt(small[b][b]), final)
        chunks[g] = jnp.where(lane <= sub + base, final, jnp.float32(0.0))
    return jnp.concatenate(chunks, axis=0)


def add_diagonal(work, prior, damping):
    order = work.shape[0]
    rows = lax.broadcasted_iota(jnp.int32, (PANEL, PANEL), 0)
    columns = lax.broadcasted_iota(jnp.int32, (PANEL, PANEL), 1)
    for q in range(order // PANEL):
        at = q * PANEL
        extra = jnp.broadcast_to(prior[0:1, at : at + PANEL] * damping, (PANEL, PANEL))
        tile = work[at : at + PANEL, at : at + PANEL]
        work[at : at + PANEL, at : at + PANEL] = tile + jnp.where(rows == columns, extra, F32(0.0))


def back_substitute(work, inv, y):
    order = work.shape[0]
    for q in reversed(range(order // PANEL)):
        at = q * PANEL
        current = y[:, at : at + PANEL]
        if at + PANEL < order:
            current = current - dot_nt(y[:, at + PANEL : order], work[at : at + PANEL, at + PANEL : order])
        y[:, at : at + PANEL] = dot_nn(current, inv[at : at + PANEL, :])


def eliminate(work, inv, y, before, after):
    order = work.shape[0]
    count = order // PANEL

    def panel(p, carry):
        for q in range(count):

            @pl.when(p == q)
            def update(q=q):
                before(q)
                at = q * PANEL
                if q > 0:
                    above = work[0:at, at : at + PANEL]
                    work[at : at + PANEL, at:] = work[at : at + PANEL, at:] - dot_tn(above, work[0:at, at:])
                    if y is not None:
                        y[:, at : at + PANEL] = y[:, at : at + PANEL] - dot_nn(y[:, 0:at], above)

        at = pl.multiple_of(p * PANEL, PANEL)
        inv[pl.ds(at, PANEL), :] = inverse_factor(work[pl.ds(at, PANEL), pl.ds(at, PANEL)])
        for q in range(count):

            @pl.when(p == q)
            def apply(q=q):
                after(q)
                at = q * PANEL
                own = inv[at : at + PANEL, :]
                if at + PANEL < order:
                    work[at : at + PANEL, at + PANEL :] = dot_nn(own, work[at : at + PANEL, at + PANEL :])
                if y is not None:
                    y[:, at : at + PANEL] = dot_nt(y[:, at : at + PANEL], own)

        return carry

    lax.fori_loop(0, count, panel, 0)


def forward(work, inv, block, y):
    for q in range(work.shape[0] // PANEL):
        at = q * PANEL
        own = inv[at : at + PANEL, :]
        value, vector = block[at : at + PANEL, :], y[:, at : at + PANEL]
        if q > 0:
            above = work[0:at, at : at + PANEL]
            value = value - dot_tn(above, block[0:at, :])
            vector = vector - dot_nn(y[:, 0:at], above)
        block[at : at + PANEL, :] = dot_nn(own, value)
        y[:, at : at + PANEL] = dot_nt(vector, own)


def step_kernel(
    plan,
    n_regime,
    count_ref,
    prior_ref,
    local_ref,
    global_ref,
    index_ref,
    tap_ref,
    residual_ref,
    obs_ref,
    rprior_ref,
    gprior_ref,
    local_step,
    regional_step,
    global_step,
    rows8,
    reg_ref,
    scaled_r,
    scaled_g,
    reduced,
    work,
    inv,
    block,
    y,
    gwork,
    ginv,
    gy,
    scalars,
    vectors,
    share_send,
    share_recv,
    *pieces,
):
    barrier, total = enter(plan, n_regime)
    r, o = lax.axis_index("regime"), lax.axis_index("obj")
    nparams, width = local_ref.shape
    objects = count_ref.shape[0]
    regional_width, global_width = rprior_ref.shape[1], global_ref.shape[1]
    columns = regional_width + global_width
    rt, gt = regional_width // PANEL, global_width // PANEL
    half = rt // 2
    sections = [Section(plan, *pieces[7 * i : 7 * i + 3], pieces[7 * i + 3 : 7 * i + 7]) for i in range(5)]
    first, second, upper, lower, last = sections
    pieces = pieces[35:]
    joins = [Join(plan, n_regime, *pieces[7 * i : 7 * i + 3], pieces[7 * i + 3 : 7 * i + 7]) for i in range(gt)]
    tile = (GROUP, PANEL)

    def share(which, slot):
        return [
            pltpu.make_async_remote_copy(
                src_ref=which.at[0],
                dst_ref=which.at[k + 1],
                send_sem=share_send.at[slot, k],
                recv_sem=share_recv.at[slot, k],
                device_id=(lax.rem(r + k + 1, n_regime), o),
                device_id_type=MESH,
            )
            for k in range(n_regime - 1)
        ]

    weight, residual, misfit, counted, weighted, factor, vector = local_pieces(
        local_ref, residual_ref, obs_ref, count_ref, prior_ref, rows8
    )
    sub = lax.broadcasted_iota(jnp.int32, tile, 0)
    scalars[0] = jnp.where(sub == 0, misfit, jnp.where(sub == 1, counted, F32(0.0)))
    pl.semaphore_wait(barrier, total)
    for copy in share(scalars, 0):
        copy.start()

    shape = (regional_width, width)
    ids = lax.broadcasted_iota(jnp.int32, shape, 0)
    regional = jnp.zeros(shape, F32)
    taps = tap_ref[...].astype(F32)
    for k in range(index_ref.shape[0]):
        regional = regional + jnp.where(
            jnp.broadcast_to(index_ref[k : k + 1, :], shape) == ids,
            jnp.broadcast_to(taps[k : k + 1, :], shape),
            F32(0.0),
        )
    regional = regional.astype(BF16)
    reg_ref[...] = regional
    scaled_r[...] = (regional.astype(F32) * weight).astype(BF16)
    three = jnp.concatenate(split3(weighted), axis=0).astype(BF16)
    held = nparams * objects
    res3 = three_rows(residual, width)

    def reduce_columns(product, gradient, offset):
        coupling = product[0:held] + product[held : 2 * held] + product[2 * held : 3 * held]
        lines = []
        for at in range(0, coupling.shape[1], PANEL):
            cols = slice(at, at + PANEL)
            result = forward_small(factor, [coupling[a * objects : (a + 1) * objects, cols] for a in range(nparams)])
            dropped = vector[0] * result[0]
            for a in range(1, nparams):
                dropped = dropped + vector[a] * result[a]
            for a in range(nparams):
                reduced[a * objects : (a + 1) * objects, offset + at : offset + at + PANEL] = result[a]
            lines.append(gradient[:, cols] - jnp.sum(dropped, axis=0, keepdims=True))
        pieces = split3(reduced[:, offset : offset + coupling.shape[1]])
        left = jnp.concatenate([pieces[t] for t in (0, 0, 1, 0, 1, 2)], axis=0).astype(BF16)
        right = jnp.concatenate([pieces[t] for t in (0, 1, 0, 2, 1, 0)], axis=0).astype(BF16)
        return lines, left, right

    gradient = jnp.sum(dot_nt(res3, scaled_r[...], None), axis=0, keepdims=True)
    lines_r, left_r, right_r = reduce_columns(dot_nt(three, reg_ref[...], None), gradient, 0)

    def regional_line(i):
        own, rest = slice(i * PANEL, (i + 1) * PANEL), slice(i * PANEL, regional_width)
        line = dot_nt(scaled_r[own, :], reg_ref[rest, :], None) + dot_nt(reg_ref[own, :], scaled_r[rest, :], None)
        return 0.5 * line - dot_tn(left_r[:, own], right_r[:, rest], None)

    at = line_of_tiles(first.part, 0, regional_line(0))
    for copy in share(scalars, 0):
        copy.wait()
    both = scalars[0]
    for k in range(n_regime - 1):
        both = both + scalars[k + 1]
    first.part[at : at + GROUP, :] = both
    damp_at = at
    clear(first.part, at + GROUP)
    if plan:
        first.start()
    at = 0
    for i in range(1, rt):
        at = line_of_tiles(second.part, at, regional_line(i))
    clear(second.part, at)
    if plan:
        second.start()
        first.next()

    wide = -(-width // PANEL) * PANEL
    eight = jnp.broadcast_to(weight, (GROUP, width))
    if wide > width:
        eight = jnp.concatenate([eight, jnp.zeros((GROUP, wide - width), F32)], axis=1)
    column = jnp.transpose(eight)[:width, 0:1]
    scaled_g[...] = (global_ref[...].astype(F32) * column).astype(BF16)
    gradient = jnp.sum(dot_nn(res3, scaled_g[...], None), axis=0, keepdims=True)
    lines_g, left_g, right_g = reduce_columns(dot_nn(three, global_ref[...], None), gradient, regional_width)

    def mixed_line(i):
        own = slice(i * PANEL, (i + 1) * PANEL)
        return dot_nn(scaled_r[own, :], global_ref[...], None) - dot_tn(left_r[:, own], right_g, None)

    def global_line(i):
        own, rest = slice(i * PANEL, (i + 1) * PANEL), slice(i * PANEL, global_width)
        line = dot_tn(scaled_g[:, own], global_ref[:, rest], None) + dot_tn(global_ref[:, own], scaled_g[:, rest], None)
        return 0.5 * line - dot_tn(left_g[:, own], right_g[:, rest], None)

    at = 0
    for i in range(half):
        at = line_of_tiles(upper.part, at, mixed_line(i))
    rhs_at = at
    for c, line in enumerate(lines_r + lines_g):
        upper.part[at + c : at + c + 1, :] = line
    clear(upper.part, at + columns // PANEL)
    if plan:
        upper.start()
        second.next()
    at = 0
    for i in range(half, rt):
        at = line_of_tiles(lower.part, at, mixed_line(i))
    clear(lower.part, at)
    if plan:
        lower.start()
    at = 0
    for i in range(gt):
        at = line_of_tiles(last.part, at, global_line(i))
    clear(last.part, at)
    if plan:
        last.start()

    staged = len(plan) == 3
    if staged:
        upper.finish()
        first.next()
        upper.start()
        second.next()
        lower.finish()
        last.finish()
        first.next()
        second.next()
        first.next()
        upper.next()
        second.next()
        lower.start()
        last.start()
        first.next()
        first.finish()
    else:
        for section in sections:
            section.rest()

    scale = first.result()
    damping = scale[damp_at : damp_at + 1, :] / scale[damp_at + 1 : damp_at + 2, :]
    for j in range(rt):
        work[0:PANEL, j * PANEL : (j + 1) * PANEL] = scale[j * PANEL : (j + 1) * PANEL, :]

    def diagonal(target, prior, q):
        rows = lax.broadcasted_iota(jnp.int32, (PANEL, PANEL), 0)
        cols = lax.broadcasted_iota(jnp.int32, (PANEL, PANEL), 1)
        own = slice(q * PANEL, (q + 1) * PANEL)
        extra = jnp.broadcast_to(prior[0:1, own] * damping, (PANEL, PANEL))
        target[own, own] = target[own, own] + jnp.where(rows == cols, extra, F32(0.0))

    def before(q):
        if q == 1:
            at = 0
            for i in range(1, rt):
                for j in range(i, rt):
                    work[i * PANEL : (i + 1) * PANEL, j * PANEL : (j + 1) * PANEL] = second.result()[at : at + PANEL, :]
                    at += PANEL
        diagonal(work, rprior_ref, q)

    def after(q):
        if not staged:
            return
        if q == 0:
            second.next()
            upper.next()
            lower.next()
            last.next()
            second.finish()
        if q == 1:
            upper.next()
            lower.next()
            last.next()
        if q == 2:
            upper.next()
            lower.next()
            last.next()
        if q == rt - 1:
            upper.rest()
            lower.rest()
            last.rest()

    eliminate(work, inv, None, before, after)
    for i in range(rt):
        side, at = (upper, i * gt * PANEL) if i < half else (lower, (i - half) * gt * PANEL)
        for j in range(gt):
            block[i * PANEL : (i + 1) * PANEL, j * PANEL : (j + 1) * PANEL] = side.result()[
                at + j * PANEL : at + (j + 1) * PANEL, :
            ]
    rhs = upper.result()
    for c in range(rt):
        y[:, c * PANEL : (c + 1) * PANEL] = jnp.broadcast_to(rhs[rhs_at + c : rhs_at + c + 1, :], tile)
    forward(work, inv, block, y)
    dropped = dot_nn(y[...], block[...])
    vectors[0] = jnp.zeros(tile, F32)
    for j in range(gt):
        at = rhs_at + rt + j
        vectors[0, j : j + 1, :] = rhs[at : at + 1, :] - dropped[0:1, j * PANEL : (j + 1) * PANEL]
    for copy in share(vectors, 1):
        copy.start()
    at = 0
    for i in range(gt):
        line = dot_tn(block[:, i * PANEL : (i + 1) * PANEL], block[:, i * PANEL :])
        for j in range(gt - i):
            joins[i].part[j * PANEL : (j + 1) * PANEL, :] = (
                last.result()[at : at + PANEL, :] - line[:, j * PANEL : (j + 1) * PANEL]
            )
            at += PANEL
        joins[i].start()

    def unpack(i):
        for j in range(i, gt):
            gwork[i * PANEL : (i + 1) * PANEL, j * PANEL : (j + 1) * PANEL] = joins[i].full[
                (j - i) * PANEL : (j - i + 1) * PANEL, :
            ]

    joins[0].add()
    for copy in share(vectors, 1):
        copy.wait()
    vector_sum = None
    for g in range(n_regime):
        line = vectors[0]
        for k in range(n_regime - 1):
            line = jnp.where(lax.rem(r + n_regime - k - 1, n_regime) == g, vectors[k + 1], line)
        vector_sum = line if vector_sum is None else vector_sum + line
    for j in range(gt):
        gy[:, j * PANEL : (j + 1) * PANEL] = jnp.broadcast_to(vector_sum[j : j + 1, :], tile)
    joins[0].finish()

    def before_global(q):
        if q > 0:
            joins[q].finish()
        unpack(q)
        diagonal(gwork, gprior_ref, q)

    def after_global(q):
        if q == 0:
            for join in joins[1:]:
                join.add()

    eliminate(gwork, ginv, gy, before_global, after_global)
    back_substitute(gwork, ginv, gy)
    global_step[...] = gy[0:1, :]
    y[...] = y[...] - dot_nt(gy[...], block[...])
    back_substitute(work, inv, y)
    regional_step[...] = y[0:1, :]

    moved = dot_nn(three_rows(y[0:1, :], regional_width), reg_ref[...], None)
    moved = moved + dot_nt(three_rows(gy[0:1, :], global_width), global_ref[...], None)
    moved = jnp.sum(moved, axis=0, keepdims=True)
    target = jnp.sum(weighted * (residual - moved), axis=1, keepdims=True)
    vreg = (objects, PANEL)
    targets = [jnp.broadcast_to(target[a * objects : (a + 1) * objects, :], vreg) for a in range(nparams)]
    solved = backward_small(factor, forward_small(factor, targets))
    lane = lax.broadcasted_iota(jnp.int32, vreg, 1)
    side = jnp.zeros(vreg, F32)
    for a in range(nparams):
        side = jnp.where(lane == a, solved[a], side)
    local_step[...] = jnp.transpose(side)[0:nparams, 0:objects]


def vmem(count):
    return [pl.BlockSpec(memory_space=pltpu.VMEM)] * count


def smem(count):
    return [pl.BlockSpec(memory_space=pltpu.SMEM)] * count


def body(
    n_regime,
    n_obj,
    local_jac,
    global_jac,
    coeff_index,
    coeff_weight,
    residual,
    obs_weight,
    obs_count,
    local_prior,
    regional_prior,
    global_prior,
):
    nparams, width = local_jac.shape
    objects = obs_count.shape[0]
    regional_width, order = regional_prior.shape[1], global_jac.shape[1]
    rt, gt = regional_width // PANEL, order // PANEL
    half = rt // 2
    plan = stage_plan(n_obj)
    columns = regional_width + order
    peers = max(n_regime - 1, 1)

    def buffer(*shape, dtype=F32):
        return pltpu.VMEM(shape, dtype)

    sections = [
        rt * PANEL + GROUP,
        rt * (rt - 1) // 2 * PANEL,
        half * gt * PANEL + columns // PANEL,
        (rt - half) * gt * PANEL,
        gt * (gt + 1) // 2 * PANEL,
    ]
    scratch = [
        buffer(nparams + 1, width),
        buffer(regional_width, width, dtype=BF16),
        buffer(regional_width, width, dtype=BF16),
        buffer(width, order, dtype=BF16),
        buffer(nparams * objects, columns),
        buffer(regional_width, regional_width),
        buffer(regional_width, PANEL),
        buffer(regional_width, order),
        buffer(GROUP, regional_width),
        buffer(order, order),
        buffer(order, PANEL),
        buffer(GROUP, order),
        buffer(n_regime, GROUP, PANEL),
        buffer(n_regime, GROUP, PANEL),
        pltpu.SemaphoreType.DMA((2, peers)),
        pltpu.SemaphoreType.DMA((2, peers)),
    ]
    for rows in sections:
        scratch += section_scratch(padded(rows, n_obj), plan)
    for i in range(gt):
        scratch += join_scratch((gt - i) * PANEL, plan, n_regime)
    shapes = ((nparams, objects), (1, regional_width), (1, order))
    local_step, regional_step, global_step = pl.pallas_call(
        functools.partial(step_kernel, plan, n_regime),
        out_shape=tuple(jax.ShapeDtypeStruct(shape, F32) for shape in shapes),
        in_specs=smem(2) + vmem(8),
        out_specs=tuple(vmem(3)),
        scratch_shapes=scratch,
        compiler_params=pltpu.CompilerParams(collective_id=0, has_side_effects=True),
        name="step",
    )(
        obs_count,
        local_prior,
        local_jac,
        global_jac,
        coeff_index,
        coeff_weight,
        residual[None, :],
        obs_weight[None, :],
        regional_prior,
        global_prior[None, :],
    )
    return (local_step, regional_step, global_step[0])


def solution(mesh):
    return jax.shard_map(
        functools.partial(body, mesh.shape["regime"], mesh.shape["obj"]),
        mesh=mesh,
        in_specs=(
            P(None, ("regime", "obj")),
            P(("regime", "obj"), None),
            P(None, ("regime", "obj")),
            P(None, ("regime", "obj")),
            P(("regime", "obj")),
            P(("regime", "obj")),
            P(("regime", "obj")),
            P(None, ("regime", "obj")),
            P("regime", None),
            P(),
        ),
        out_specs=(P(None, ("regime", "obj")), P("regime", None), P()),
        check_vma=False,
    )
```

time: 353 us -> 102 us (0.29)
  waiting for transfers between devices: 190 us -> 0 us
  Pallas kernels: 55.3 us -> 98.1 us
  blocking collectives: 42.6 us -> 0 us
  local copies, waits for them, and re-layouts: 22.6 us -> 2.59 us
  other arithmetic: 19.1 us -> 0 us
  between operations: 15.4 us -> 0.65 us
  matrix products: 7.32 us -> 0 us
    psum x3 -> x0, waiting for transfers between devices: 190 us -> none  [the longest x1 95.3 us: body(): global_block = lax.psum(schur[width:, width:], ('regime', 'obj'))]
    pallas_call x2 -> x1, Pallas kernels: 55.3 us -> 98.1 us  [body(): pl.pallas_call(functools.partial(step_kernel, plan, n_regime), out_shape=...]
    psum x1 -> x0, blocking collectives: 42.6 us -> none  [body(): lax.psum((jnp.sum(weight * residual * residual), jnp.sum(present.astype(j...]
    slice x17 -> x0, local copies, waits for them, and re-layouts: 13.5 us -> none  [the longest x3 5.55 us: body(): regional_block, block = (upper[:width, :width], upper[:width, width:])]
    dot_general x7 -> x0, matrix products: 7.32 us -> none  [the longest x1 3.52 us: body(): jnp.dot(stacked.T, stacked, precision=lax.Precision.HIGHEST)]
    concatenate x5 -> x0, other arithmetic: 5.87 us -> none  [the longest x1 2.79 us: body(): upper = jnp.concatenate([schur[:width], rhs.reshape(1, -1)], axis=0)]
    add x2 -> x0, other arithmetic: 3.86 us -> none  [the longest x1 2.43 us: body(): global_block + reduced_global[:-1]]
  transfers between devices with their start and end apart: 3 -> 0, of which waited for: 3 -> 0; matrix products, arithmetic and copies ran while one was open for 6% -> 0% of each run, Pallas kernels for 8% -> 0%
where the time goes in v2:
time: 102 us; the launch traced here: 101 us
  Pallas kernels  98.1 us (96%)
  local copies, waits for them, and re-layouts  2.59 us (3%)
    pallas_call x1, Pallas kernels, body(): pl.pallas_call(functools.partial(step_kernel, plan, n_regime), out_shape=...  98.1 us
    unnamed x9, local copies, waits for them, and re-layouts  2.59 us

profile of v2, /device:TPU:0, one launch (start us, length us, event | category | flops | bytes accessed | tf_op | source)
XLA Modules:
  0.0 101.3 jit_solution(15059610329768846013)
XLA Ops:
  0.6 98.1 %step.1 = (f32[7,8]{1,0:T(8,128)}, f32[1,512]{1,0:T(1,128)}, f32[1,512]{1,0:T(1,128)}) custom-call(s32[8]{0:T(128)} %count_ref.1, f32[7,8]{1,0:T(8,128)} %prior_ref.1, bf16[7,480]{1,0:T(8,128)(2,1)} %local_ref.1, bf16[480,512]{1,0:T(8,128)(2,1)} %global_ref.1, s32[4,480]{1,0:T(4,128)} %index_ref.1, bf16[4,480]{1,0:T(4,128)(2,1)} %tap_ref.1, ...), custom_call_target="tpu_custom_call" | custom-call | tf_op jit(solution)/shard_map/step/pallas_call | solution.py:850
  98.7 0.0 copy-start
  98.7 0.7 copy-done
  99.4 0.0 copy-start.2
  99.4 0.6 copy.16
  100.0 0.1 copy-done.2
  100.0 0.0 copy-start.1
  100.0 0.6 copy.17
  100.6 0.1 copy-done.1
  100.7 0.6 copy.18
Async XLA Ops:
  98.7 0.7 copy-start
  99.4 0.7 copy-start.2
  100.0 0.7 copy-start.1

commit v3 on v2

--- a/solution.py
+++ b/solution.py
@@ -37,11 +37,11 @@
     return [(i, j) for i in range(count) for j in range(i, count)]
 
 
-def stage_plan(count):
+def stage_plan(count, pairs=True):
     plan, stride = [], 1
     while stride < count:
         left = count // stride
-        if stride < 4 and left % 2 == 0:
+        if pairs and stride < 4 and left % 2 == 0:
             radix = 2
         elif left % 4 == 0:
             radix = 4
@@ -65,14 +65,6 @@
     digit = digit_of(o, radix, stride)
     other = lax.rem(digit + k + 1, radix)
     return o + (other - digit) * stride, digit, other
-
-
-def owned_base(o, rows, plan):
-    base, size = 0, rows
-    for radix, stride in plan:
-        size = size // radix
-        base = base + digit_of(o, radix, stride) * size
-    return base
 
 
 def enter(plan, n_regime):
@@ -110,9 +102,7 @@
             gathers.append(("gather", stage, to, None, own, sub, None))
             used += (radix - 1) * sub
             base, size = own, sub
-        self.own, self.size = base, size
         self.steps += gathers[::-1]
-        self.at = 0
 
     def copies(self, at):
         kind, stage, to, there, own, sub, used = self.steps[at]
@@ -137,14 +127,14 @@
             )
         return result
 
-    def start(self):
-        for copy in self.copies(self.at):
+    def start(self, at):
+        for copy in self.copies(at):
             copy.start()
 
-    def finish(self):
-        for copy in self.copies(self.at):
+    def finish(self, at):
+        for copy in self.copies(at):
             copy.wait()
-        kind, stage, to, there, own, sub, used = self.steps[self.at]
+        kind, stage, to, there, own, sub, used = self.steps[at]
         if kind == "scatter":
             rows = pl.ds(own, sub)
             total = self.part[rows, :]
@@ -152,19 +142,44 @@
                 total = total + self.recv[used + k * sub : used + (k + 1) * sub, :]
             target = self.full if stage == len(self.plan) - 1 else self.part
             target[rows, :] = total
-        self.at += 1
-
-    def next(self):
-        self.finish()
-        if self.at < len(self.steps):
-            self.start()
-
-    def rest(self):
-        while self.at < len(self.steps):
-            self.next()
+        if at + 1 < len(self.steps):
+            self.start(at + 1)
 
     def result(self):
         return self.full if self.plan else self.part
+
+
+SCRIPT = {
+    "C4a": "1",
+    "C4b": "0AB",
+    "upd0": "L1A0UBG1A0UB1LAGV10M",
+    "inv0.2": "A",
+    "inv0.3": "V",
+    "app0": "ML1BUA",
+    "inv1.3": "BV",
+    "upd2": "BMG",
+    "inv2.1": "L",
+    "inv2.3": "U",
+    "inv3.0": "V",
+    "inv3.2": "ML",
+    "inv3.3": "U",
+    "X0": "VLU",
+    "X1": "GVM",
+    "X3": "M",
+    "join": "GG",
+}
+
+
+def schedule(sections, staged):
+    if not staged:
+        return {"upd0": [(x, at) for x in sections.values() for at in range(len(x.steps))]}
+    places, reached = {}, {name: 0 for name in sections}
+    for place, names in SCRIPT.items():
+        places[place] = []
+        for name in names:
+            places[place].append((sections[name], reached[name]))
+            reached[name] += 1
+    return places
 
 
 class Join:
@@ -348,54 +363,77 @@
         target[at:, :] = jnp.zeros((target.shape[0] - at, PANEL), F32)
 
 
-def inverse_factor(block):
-    order = block.shape[0]
-    lane = lax.broadcasted_iota(jnp.int32, (GROUP, order), 1)
-    sub = lax.broadcasted_iota(jnp.int32, (GROUP, order), 0)
+def inverse_factor(panel, spread, pause=None):
+    order = panel.shape[0]
     shape = (GROUP, order)
-    chunks = [block[i * GROUP : (i + 1) * GROUP, :] for i in range(order // GROUP)]
-    for g in range(order // GROUP):
+    lane = lax.broadcasted_iota(jnp.int32, shape, 1)
+    sub = lax.broadcasted_iota(jnp.int32, shape, 0)
+    count = order // GROUP
+    if pause is not None:
+        pause(-1)
+    for g in range(count):
         base = g * GROUP
         inside = (lane >= base) & (lane < base + GROUP)
-        cols = {
-            i: [jnp.broadcast_to(chunks[i][:, base + b : base + b + 1], shape) for b in range(GROUP)]
-            for i in range(g, len(chunks))
-        }
+        own = panel[base : base + GROUP, :]
+        for b in range(GROUP):
+            spread[b * GROUP : (b + 1) * GROUP, :] = jnp.broadcast_to(own[:, base + b : base + b + 1], shape)
+        full = [panel[pl.ds(base + b, GROUP, stride=0), :] for b in range(GROUP)]
         small = [
-            [jnp.broadcast_to(cols[g][b][a : a + 1, :], shape) if a >= b else None for b in range(GROUP)]
-            for a in range(GROUP)
+            [spread[pl.ds(b * GROUP + a, GROUP, stride=0), :] for b in range(a + 1)] for a in range(GROUP)
         ]
         rows = [
-            jnp.where(
-                lane == base + b,
-                jnp.float32(1.0),
-                jnp.where(inside, jnp.float32(0.0), jnp.broadcast_to(chunks[g][b : b + 1, :], shape)),
-            )
-            for b in range(GROUP)
+            jnp.where(lane == base + b, F32(1.0), jnp.where(inside, F32(0.0), full[b])) for b in range(GROUP)
         ]
-        inverse = []
-        for b in range(GROUP):
-            recip = 1.0 / small[b][b]
-            inverse.append(recip)
-            ratio = [small[a][b] * recip if a > b else None for a in range(GROUP)]
-            for a in range(b + 1, GROUP):
-                rows[a] = rows[a] - ratio[a] * rows[b]
-                for c in range(b + 1, a + 1):
-                    small[a][c] = small[a][c] - ratio[a] * small[c][b]
-            for i in range(g + 1, len(chunks)):
-                for c in range(b + 1, GROUP):
-                    cols[i][c] = cols[i][c] - cols[i][b] * ratio[c]
-        scaled_rows = [rows[b] * inverse[b] for b in range(GROUP)]
-        for i in range(g + 1, len(chunks)):
-            current = jnp.where(inside, jnp.float32(0.0), chunks[i])
-            for b in range(GROUP):
-                current = current - cols[i][b] * scaled_rows[b]
-            chunks[i] = current
-        final = jnp.zeros(shape, jnp.float32)
-        for b in range(GROUP):
-            final = jnp.where(sub == b, rows[b] / jnp.sqrt(small[b][b]), final)
-        chunks[g] = jnp.where(lane <= sub + base, final, jnp.float32(0.0))
-    return jnp.concatenate(chunks, axis=0)
+        final = jnp.zeros(shape, F32)
+        solved, factors = [None] * GROUP, {}
+
+        def columns(i):
+            chunk = panel[i * GROUP : (i + 1) * GROUP, :]
+            cols = [jnp.broadcast_to(chunk[:, base + b : base + b + 1], shape) for b in range(GROUP)]
+            return jnp.where(inside, F32(0.0), chunk), cols
+
+        near = columns(g + 1)[1] if g + 1 < count else None
+        for k in range(0, GROUP, 2):
+            p, q, r = small[k][k], small[k + 1][k], small[k + 1][k + 1]
+            det = p * r - q * q
+            inverse = 1.0 / det
+            for i in range(k + 2, GROUP):
+                one = r * small[i][k] - q * small[i][k + 1]
+                two = p * small[i][k + 1] - q * small[i][k]
+                for j in range(k + 2, i + 1):
+                    small[i][j] = small[i][j] - inverse * (one * small[j][k] + two * small[j][k + 1])
+                one, two = one * inverse, two * inverse
+                factors[i, k] = (one, two)
+                rows[i] = rows[i] - (one * rows[k] + two * rows[k + 1])
+                if near is not None:
+                    near[i] = near[i] - (one * near[k] + two * near[k + 1])
+            lead = p * rows[k + 1] - q * rows[k]
+            solved[k] = (r * rows[k] - q * rows[k + 1]) * inverse
+            solved[k + 1] = lead * inverse
+            root = lax.rsqrt(p)
+            final = jnp.where(sub == k, rows[k] * root, final)
+            final = jnp.where(sub == k + 1, lead * (root * lax.rsqrt(det)), final)
+        if g + 1 < count:
+            i = g + 1
+            terms = [near[b] * solved[b] for b in range(GROUP)]
+            while len(terms) > 1:
+                terms = [terms[t] + terms[t + 1] for t in range(0, len(terms), 2)]
+            panel[i * GROUP : (i + 1) * GROUP, :] = columns(i)[0] - terms[0]
+        if g + 2 < count:
+            for k in range(GROUP - 4, -1, -2):
+                for i in range(k + 2, GROUP):
+                    one, two = factors[i, k]
+                    solved[k] = solved[k] - one * solved[i]
+                    solved[k + 1] = solved[k + 1] - two * solved[i]
+        for i in range(g + 2, count):
+            chunk, cols = columns(i)
+            terms = [cols[b] * solved[b] for b in range(GROUP)]
+            while len(terms) > 1:
+                terms = [terms[t] + terms[t + 1] for t in range(0, len(terms), 2)]
+            panel[i * GROUP : (i + 1) * GROUP, :] = chunk - terms[0]
+        panel[base : base + GROUP, :] = jnp.where(lane <= sub + base, final, F32(0.0))
+        if pause is not None:
+            pause(g)
 
 
 def add_diagonal(work, prior, damping):
@@ -419,7 +457,7 @@
         y[:, at : at + PANEL] = dot_nn(current, inv[at : at + PANEL, :])
 
 
-def eliminate(work, inv, y, before, after):
+def eliminate(work, inv, y, before, after, panel_ref, spread_ref, pause=None):
     order = work.shape[0]
     count = order // PANEL
 
@@ -437,7 +475,9 @@
                         y[:, at : at + PANEL] = y[:, at : at + PANEL] - dot_nn(y[:, 0:at], above)
 
         at = pl.multiple_of(p * PANEL, PANEL)
-        inv[pl.ds(at, PANEL), :] = inverse_factor(work[pl.ds(at, PANEL), pl.ds(at, PANEL)])
+        panel_ref[...] = work[pl.ds(at, PANEL), pl.ds(at, PANEL)]
+        inverse_factor(panel_ref, spread_ref, None if pause is None else functools.partial(pause, p))
+        inv[pl.ds(at, PANEL), :] = panel_ref[...]
         for q in range(count):
 
             @pl.when(p == q)
@@ -455,21 +495,21 @@
     lax.fori_loop(0, count, panel, 0)
 
 
-def forward(work, inv, block, y):
-    for q in range(work.shape[0] // PANEL):
-        at = q * PANEL
-        own = inv[at : at + PANEL, :]
-        value, vector = block[at : at + PANEL, :], y[:, at : at + PANEL]
-        if q > 0:
-            above = work[0:at, at : at + PANEL]
-            value = value - dot_tn(above, block[0:at, :])
-            vector = vector - dot_nn(y[:, 0:at], above)
-        block[at : at + PANEL, :] = dot_nn(own, value)
-        y[:, at : at + PANEL] = dot_nt(vector, own)
+def forward(work, inv, block, y, q):
+    at = q * PANEL
+    own = inv[at : at + PANEL, :]
+    value, vector = block[at : at + PANEL, :], y[:, at : at + PANEL]
+    if q > 0:
+        above = work[0:at, at : at + PANEL]
+        value = value - dot_tn(above, block[0:at, :])
+        vector = vector - dot_nn(y[:, 0:at], above)
+    block[at : at + PANEL, :] = dot_nn(own, value)
+    y[:, at : at + PANEL] = dot_nt(vector, own)
 
 
 def step_kernel(
     plan,
+    wide_plan,
     n_regime,
     count_ref,
     prior_ref,
@@ -485,6 +525,8 @@
     regional_step,
     global_step,
     rows8,
+    panel_ref,
+    spread_ref,
     reg_ref,
     scaled_r,
     scaled_g,
@@ -502,18 +544,32 @@
     share_recv,
     *pieces,
 ):
-    barrier, total = enter(plan, n_regime)
+    barrier, total = enter(wide_plan, n_regime)
     r, o = lax.axis_index("regime"), lax.axis_index("obj")
     nparams, width = local_ref.shape
     objects = count_ref.shape[0]
     regional_width, global_width = rprior_ref.shape[1], global_ref.shape[1]
     columns = regional_width + global_width
     rt, gt = regional_width // PANEL, global_width // PANEL
-    half = rt // 2
-    sections = [Section(plan, *pieces[7 * i : 7 * i + 3], pieces[7 * i + 3 : 7 * i + 7]) for i in range(5)]
-    first, second, upper, lower, last = sections
-    pieces = pieces[35:]
+    names = "01ABUVLMG"
+    sections = {}
+    for i, name in enumerate(names):
+        held = pieces[7 * i : 7 * i + 7]
+        sections[name] = Section(wide_plan if name == "0" else plan, *held[:3], held[3:])
+    pieces = pieces[7 * len(names) :]
     joins = [Join(plan, n_regime, *pieces[7 * i : 7 * i + 3], pieces[7 * i + 3 : 7 * i + 7]) for i in range(gt)]
+    staged = rt == 4 and gt == 4 and [radix for radix, _ in plan] == [2, 2, 4]
+    places = schedule(sections, staged)
+
+    def progress(place):
+        for section, at in places.get(place, ()):
+            section.finish(at)
+
+    def begin(name, rows):
+        clear(sections[name].part, rows)
+        if plan:
+            sections[name].start(0)
+
     tile = (GROUP, PANEL)
 
     def share(which, slot):
@@ -575,29 +631,30 @@
     gradient = jnp.sum(dot_nt(res3, scaled_r[...], None), axis=0, keepdims=True)
     lines_r, left_r, right_r = reduce_columns(dot_nt(three, reg_ref[...], None), gradient, 0)
 
-    def regional_line(i):
-        own, rest = slice(i * PANEL, (i + 1) * PANEL), slice(i * PANEL, regional_width)
+    def regional_line(i, start, end):
+        own, rest = slice(i * PANEL, (i + 1) * PANEL), slice(start * PANEL, end * PANEL)
         line = dot_nt(scaled_r[own, :], reg_ref[rest, :], None) + dot_nt(reg_ref[own, :], scaled_r[rest, :], None)
         return 0.5 * line - dot_tn(left_r[:, own], right_r[:, rest], None)
 
-    at = line_of_tiles(first.part, 0, regional_line(0))
+    corner = sections["0"]
+    corner.part[0:PANEL, :] = regional_line(0, 0, 1)
     for copy in share(scalars, 0):
         copy.wait()
     both = scalars[0]
     for k in range(n_regime - 1):
         both = both + scalars[k + 1]
-    first.part[at : at + GROUP, :] = both
-    damp_at = at
-    clear(first.part, at + GROUP)
-    if plan:
-        first.start()
+    last = PANEL - 1
+    lane = lax.broadcasted_iota(jnp.int32, (1, PANEL), 1)
+    corner.part[last:PANEL, :] = jnp.where(
+        lane == 0, both[0:1, :], jnp.where(lane == 1, both[1:2, :], corner.part[last:PANEL, :])
+    )
+    begin("0", PANEL)
+    begin("1", line_of_tiles(sections["1"].part, 0, regional_line(0, 1, rt)))
+    begin("A", line_of_tiles(sections["A"].part, 0, regional_line(1, 1, rt)))
     at = 0
-    for i in range(1, rt):
-        at = line_of_tiles(second.part, at, regional_line(i))
-    clear(second.part, at)
-    if plan:
-        second.start()
-        first.next()
+    for i in range(2, rt):
+        at = line_of_tiles(sections["B"].part, at, regional_line(i, i, rt))
+    begin("B", at)
 
     wide = -(-width // PANEL) * PANEL
     eight = jnp.broadcast_to(weight, (GROUP, width))
@@ -617,54 +674,31 @@
         line = dot_tn(scaled_g[:, own], global_ref[:, rest], None) + dot_tn(global_ref[:, own], scaled_g[:, rest], None)
         return 0.5 * line - dot_tn(left_g[:, own], right_g[:, rest], None)
 
+    progress("C4a")
+    rhs_at = line_of_tiles(sections["U"].part, 0, mixed_line(0))
+    for c, line in enumerate(lines_r + lines_g):
+        sections["U"].part[rhs_at + c : rhs_at + c + 1, :] = line
+    begin("U", rhs_at + columns // PANEL)
+    progress("C4b")
+    begin("V", line_of_tiles(sections["V"].part, 0, mixed_line(1)))
+    progress("C5a")
+    begin("L", line_of_tiles(sections["L"].part, 0, mixed_line(2)))
+    progress("C5b")
     at = 0
-    for i in range(half):
-        at = line_of_tiles(upper.part, at, mixed_line(i))
-    rhs_at = at
-    for c, line in enumerate(lines_r + lines_g):
-        upper.part[at + c : at + c + 1, :] = line
-    clear(upper.part, at + columns // PANEL)
-    if plan:
-        upper.start()
-        second.next()
-    at = 0
-    for i in range(half, rt):
-        at = line_of_tiles(lower.part, at, mixed_line(i))
-    clear(lower.part, at)
-    if plan:
-        lower.start()
+    for i in range(3, rt):
+        at = line_of_tiles(sections["M"].part, at, mixed_line(i))
+    begin("M", at)
+    progress("C6")
     at = 0
     for i in range(gt):
-        at = line_of_tiles(last.part, at, global_line(i))
-    clear(last.part, at)
-    if plan:
-        last.start()
-
-    staged = len(plan) == 3
-    if staged:
-        upper.finish()
-        first.next()
-        upper.start()
-        second.next()
-        lower.finish()
-        last.finish()
-        first.next()
-        second.next()
-        first.next()
-        upper.next()
-        second.next()
-        lower.start()
-        last.start()
-        first.next()
-        first.finish()
-    else:
-        for section in sections:
-            section.rest()
-
-    scale = first.result()
-    damping = scale[damp_at : damp_at + 1, :] / scale[damp_at + 1 : damp_at + 2, :]
-    for j in range(rt):
-        work[0:PANEL, j * PANEL : (j + 1) * PANEL] = scale[j * PANEL : (j + 1) * PANEL, :]
+        at = line_of_tiles(sections["G"].part, at, global_line(i))
+    begin("G", at)
+    progress("upd0")
+
+    sums = corner.result()[last:PANEL, :]
+    damping = jnp.broadcast_to(sums[:, 0:1], (1, PANEL)) / jnp.broadcast_to(sums[:, 1:2], (1, PANEL))
+    work[0:PANEL, 0:PANEL] = corner.result()[0:PANEL, :]
+    work[last:PANEL, 0:PANEL] = jnp.transpose(corner.result()[0:PANEL, :])[last:PANEL, :]
 
     def diagonal(target, prior, q):
         rows = lax.broadcasted_iota(jnp.int32, (PANEL, PANEL), 0)
@@ -673,48 +707,51 @@
         extra = jnp.broadcast_to(prior[0:1, own] * damping, (PANEL, PANEL))
         target[own, own] = target[own, own] + jnp.where(rows == cols, extra, F32(0.0))
 
+    def unpack_row(name, i, start, at=0):
+        for j in range(start, rt):
+            work[i * PANEL : (i + 1) * PANEL, j * PANEL : (j + 1) * PANEL] = sections[name].result()[at : at + PANEL, :]
+            at += PANEL
+        return at
+
     def before(q):
+        if q > 0:
+            progress(f"upd{q}")
         if q == 1:
+            unpack_row("A", 1, 1)
+        if q == 2:
             at = 0
-            for i in range(1, rt):
-                for j in range(i, rt):
-                    work[i * PANEL : (i + 1) * PANEL, j * PANEL : (j + 1) * PANEL] = second.result()[at : at + PANEL, :]
-                    at += PANEL
+            for i in range(2, rt):
+                at = unpack_row("B", i, i, at)
         diagonal(work, rprior_ref, q)
 
+    def pause(p, g):
+        quarter = PANEL // GROUP // 4
+        if (g + 1) % quarter or (g + 1) // quarter == 4:
+            return
+        for q in range(rt):
+            place = f"inv{q}.{(g + 1) // quarter}"
+            if place in places:
+                pl.when(p == q)(functools.partial(progress, place))
+
     def after(q):
-        if not staged:
-            return
+        progress(f"app{q}")
         if q == 0:
-            second.next()
-            upper.next()
-            lower.next()
-            last.next()
-            second.finish()
-        if q == 1:
-            upper.next()
-            lower.next()
-            last.next()
-        if q == 2:
-            upper.next()
-            lower.next()
-            last.next()
-        if q == rt - 1:
-            upper.rest()
-            lower.rest()
-            last.rest()
-
-    eliminate(work, inv, None, before, after)
+            unpack_row("1", 0, 1)
+
+    eliminate(work, inv, None, before, after, panel_ref, spread_ref, pause)
     for i in range(rt):
-        side, at = (upper, i * gt * PANEL) if i < half else (lower, (i - half) * gt * PANEL)
+        progress(f"X{i}")
+        name, at = ("UVL"[i], 0) if i < 3 else ("M", (i - 3) * gt * PANEL)
+        own = slice(i * PANEL, (i + 1) * PANEL)
         for j in range(gt):
-            block[i * PANEL : (i + 1) * PANEL, j * PANEL : (j + 1) * PANEL] = side.result()[
-                at + j * PANEL : at + (j + 1) * PANEL, :
-            ]
-    rhs = upper.result()
-    for c in range(rt):
-        y[:, c * PANEL : (c + 1) * PANEL] = jnp.broadcast_to(rhs[rhs_at + c : rhs_at + c + 1, :], tile)
-    forward(work, inv, block, y)
+            block[own, j * PANEL : (j + 1) * PANEL] = sections[name].result()[at : at + PANEL, :]
+            at += PANEL
+        if i == 0:
+            rhs = sections["U"].result()
+            for c in range(rt):
+                y[:, c * PANEL : (c + 1) * PANEL] = jnp.broadcast_to(rhs[rhs_at + c : rhs_at + c + 1, :], tile)
+        forward(work, inv, block, y, i)
+    rhs = sections["U"].result()
     dropped = dot_nn(y[...], block[...])
     vectors[0] = jnp.zeros(tile, F32)
     for j in range(gt):
@@ -722,14 +759,15 @@
         vectors[0, j : j + 1, :] = rhs[at : at + 1, :] - dropped[0:1, j * PANEL : (j + 1) * PANEL]
     for copy in share(vectors, 1):
         copy.start()
+    for i in range(gt):
+        line = dot_tn(block[:, i * PANEL : (i + 1) * PANEL], block[:, i * PANEL :])
+        line_of_tiles(joins[i].part, 0, line)
+    progress("join")
     at = 0
     for i in range(gt):
-        line = dot_tn(block[:, i * PANEL : (i + 1) * PANEL], block[:, i * PANEL :])
-        for j in range(gt - i):
-            joins[i].part[j * PANEL : (j + 1) * PANEL, :] = (
-                last.result()[at : at + PANEL, :] - line[:, j * PANEL : (j + 1) * PANEL]
-            )
-            at += PANEL
+        size = joins[i].part.shape[0]
+        joins[i].part[...] = sections["G"].result()[at : at + size, :] - joins[i].part[...]
+        at += size
         joins[i].start()
 
     def unpack(i):
@@ -762,7 +800,7 @@
             for join in joins[1:]:
                 join.add()
 
-    eliminate(gwork, ginv, gy, before_global, after_global)
+    eliminate(gwork, ginv, gy, before_global, after_global, panel_ref, spread_ref)
     back_substitute(gwork, ginv, gy)
     global_step[...] = gy[0:1, :]
     y[...] = y[...] - dot_nt(gy[...], block[...])
@@ -809,8 +847,7 @@
     objects = obs_count.shape[0]
     regional_width, order = regional_prior.shape[1], global_jac.shape[1]
     rt, gt = regional_width // PANEL, order // PANEL
-    half = rt // 2
-    plan = stage_plan(n_obj)
+    plan, wide_plan = stage_plan(n_obj), stage_plan(n_obj, pairs=False)
     columns = regional_width + order
     peers = max(n_regime - 1, 1)
 
@@ -818,14 +855,22 @@
         return pltpu.VMEM(shape, dtype)
 
     sections = [
-        rt * PANEL + GROUP,
-        rt * (rt - 1) // 2 * PANEL,
-        half * gt * PANEL + columns // PANEL,
-        (rt - half) * gt * PANEL,
-        gt * (gt + 1) // 2 * PANEL,
+        1,
+        rt - 1,
+        rt - 1,
+        (rt - 1) * (rt - 2) // 2,
+        gt,
+        gt,
+        gt,
+        (rt - 3) * gt,
+        gt * (gt + 1) // 2,
     ]
+    sections = [tiles * PANEL for tiles in sections]
+    sections[4] += columns // PANEL
     scratch = [
         buffer(nparams + 1, width),
+        buffer(PANEL, PANEL),
+        buffer(GROUP * GROUP, PANEL),
         buffer(regional_width, width, dtype=BF16),
         buffer(regional_width, width, dtype=BF16),
         buffer(width, order, dtype=BF16),
@@ -842,13 +887,13 @@
         pltpu.SemaphoreType.DMA((2, peers)),
         pltpu.SemaphoreType.DMA((2, peers)),
     ]
-    for rows in sections:
-        scratch += section_scratch(padded(rows, n_obj), plan)
+    for i, rows in enumerate(sections):
+        scratch += section_scratch(padded(rows, n_obj), plan if i else wide_plan)
     for i in range(gt):
         scratch += join_scratch((gt - i) * PANEL, plan, n_regime)
     shapes = ((nparams, objects), (1, regional_width), (1, order))
     local_step, regional_step, global_step = pl.pallas_call(
-        functools.partial(step_kernel, plan, n_regime),
+        functools.partial(step_kernel, plan, wide_plan, n_regime),
         out_shape=tuple(jax.ShapeDtypeStruct(shape, F32) for shape in shapes),
         in_specs=smem(2) + vmem(8),
         out_specs=tuple(vmem(3)),

time: 102 us -> 82.7 us (0.81)
  Pallas kernels: 98.1 us -> 79.2 us
    pallas_call x1, Pallas kernels: 98.1 us -> 79.2 us  [body(): pl.pallas_call(functools.partial(step_kernel, plan, wide_plan, n_regime),...]
where the time goes in v3:
time: 82.7 us; the launch traced here: 82.4 us
  Pallas kernels  79.2 us (96%)
  local copies, waits for them, and re-layouts  2.59 us (3%)
    pallas_call x1, Pallas kernels, body(): pl.pallas_call(functools.partial(step_kernel, plan, wide_plan, n_regime),...  79.2 us
    unnamed x9, local copies, waits for them, and re-layouts  2.59 us

profile of v3, /device:TPU:0, one launch (start us, length us, event | category | flops | bytes accessed | tf_op | source)
XLA Modules:
  0.0 82.4 jit_solution(2871915909707055629)
XLA Ops:
  0.6 79.2 %step.1 = (f32[7,8]{1,0:T(8,128)}, f32[1,512]{1,0:T(1,128)}, f32[1,512]{1,0:T(1,128)}) custom-call(s32[8]{0:T(128)} %count_ref.1, f32[7,8]{1,0:T(8,128)} %prior_ref.1, bf16[7,480]{1,0:T(8,128)(2,1)} %local_ref.1, bf16[480,512]{1,0:T(8,128)(2,1)} %global_ref.1, s32[4,480]{1,0:T(4,128)} %index_ref.1, bf16[4,480]{1,0:T(4,128)(2,1)} %tap_ref.1, ...), custom_call_target="tpu_custom_call" | custom-call | tf_op jit(solution)/shard_map/step/pallas_call | solution.py:895
  79.8 0.0 copy-start
  79.8 0.7 copy-done
  80.5 0.0 copy-start.2
  80.5 0.6 copy.16
  81.1 0.1 copy-done.2
  81.2 0.0 copy-start.1
  81.2 0.6 copy.17
  81.8 0.1 copy-done.1
  81.9 0.6 copy.18
Async XLA Ops:
  79.8 0.7 copy-start
  80.5 0.7 copy-start.2
  81.2 0.7 copy-start.1

commit v4 on v3

--- a/solution.py
+++ b/solution.py
@@ -106,21 +106,20 @@
 
     def copies(self, at):
         kind, stage, to, there, own, sub, used = self.steps[at]
+        first = sum(len(step[2]) for step in self.steps[:at])
         result = []
         for k, device in enumerate(to):
             if kind == "scatter":
                 src = self.part.at[pl.ds(there[k], sub)]
                 dst = self.recv.at[pl.ds(used + k * sub, sub)]
-                send, recv = self.sems[0], self.sems[1]
             else:
                 src = dst = self.full.at[pl.ds(own, sub)]
-                send, recv = self.sems[2], self.sems[3]
             result.append(
                 pltpu.make_async_remote_copy(
                     src_ref=src,
                     dst_ref=dst,
-                    send_sem=send.at[stage, k],
-                    recv_sem=recv.at[stage, k],
+                    send_sem=self.sems[0].at[k],
+                    recv_sem=self.sems[1].at[first + k],
                     device_id=device,
                     device_id_type=MESH,
                 )
@@ -150,23 +149,23 @@
 
 
 SCRIPT = {
-    "C4a": "1",
-    "C4b": "0AB",
-    "upd0": "L1A0UBG1A0UB1LAGV10M",
-    "inv0.2": "A",
-    "inv0.3": "V",
-    "app0": "ML1BUA",
-    "inv1.3": "BV",
-    "upd2": "BMG",
-    "inv2.1": "L",
-    "inv2.3": "U",
-    "inv3.0": "V",
-    "inv3.2": "ML",
-    "inv3.3": "U",
-    "X0": "VLU",
-    "X1": "GVM",
-    "X3": "M",
-    "join": "GG",
+    "C4a": "1A0B",
+    "upd0": "1VAU0NBV10LMAUB1LVA0H",
+    "inv0.2": "U",
+    "inv0.3": "1",
+    "app0": "AMAH1BLN",
+    "inv1.0": "V",
+    "inv1.2": "U",
+    "inv1.3": "B",
+    "upd2": "BM",
+    "inv2.2": "LHU",
+    "upd3": "NVU",
+    "inv3.1": "LM",
+    "inv3.3": "H",
+    "X1": "MLNV",
+    "X3": "HM",
+    "J0": "NH",
+    "J1": "N",
 }
 
 
@@ -234,12 +233,12 @@
             copy.wait()
 
 
-def sem_shape(plan):
-    return (max(len(plan), 1), max([radix - 1 for radix, _ in plan] + [1]))
-
-
 def section_scratch(rows, plan):
-    return [pltpu.VMEM((rows, PANEL), F32)] * 3 + [pltpu.SemaphoreType.DMA(sem_shape(plan))] * 4
+    widths = [radix - 1 for radix, _ in plan] + [1]
+    return [pltpu.VMEM((rows, PANEL), F32)] * 3 + [
+        pltpu.SemaphoreType.DMA((max(widths),)),
+        pltpu.SemaphoreType.DMA((2 * sum(widths[:-1]) or 1,)),
+    ]
 
 
 def join_scratch(rows, plan, n_regime):
@@ -447,17 +446,36 @@
         work[at : at + PANEL, at : at + PANEL] = tile + jnp.where(rows == columns, extra, F32(0.0))
 
 
-def back_substitute(work, inv, y):
+def times_row(matrix, row):
+    column = jnp.sum(matrix * row, axis=1, keepdims=True)
+    return jnp.broadcast_to(column, (matrix.shape[0], PANEL))
+
+
+def times_column(matrix, column):
+    lines = []
+    for j in range(matrix.shape[1] // PANEL):
+        lines.append(jnp.sum(matrix[:, j * PANEL : (j + 1) * PANEL] * column, axis=0, keepdims=True))
+    return lines[0] if len(lines) == 1 else jnp.concatenate(lines, axis=1)
+
+
+def forward_vector(work, inv, y, row, q):
+    own = slice(q * PANEL, (q + 1) * PANEL)
+    if q > 0:
+        row = row - times_column(work[0 : own.start, own], y[0 : own.start, :])
+    y[own, :] = times_row(inv[own, :], row)
+
+
+def back_substitute(work, inv, y, x):
     order = work.shape[0]
     for q in reversed(range(order // PANEL)):
-        at = q * PANEL
-        current = y[:, at : at + PANEL]
-        if at + PANEL < order:
-            current = current - dot_nt(y[:, at + PANEL : order], work[at : at + PANEL, at + PANEL : order])
-        y[:, at : at + PANEL] = dot_nn(current, inv[at : at + PANEL, :])
-
-
-def eliminate(work, inv, y, before, after, panel_ref, spread_ref, pause=None):
+        own = slice(q * PANEL, (q + 1) * PANEL)
+        current = y[own, :]
+        if own.stop < order:
+            current = current - times_row(work[own, own.stop : order], x[:, own.stop : order])
+        x[:, own] = times_column(inv[own, :], current)
+
+
+def eliminate(work, inv, before, after, panel_ref, spread_ref, pause=None):
     order = work.shape[0]
     count = order // PANEL
 
@@ -471,8 +489,6 @@
                 if q > 0:
                     above = work[0:at, at : at + PANEL]
                     work[at : at + PANEL, at:] = work[at : at + PANEL, at:] - dot_tn(above, work[0:at, at:])
-                    if y is not None:
-                        y[:, at : at + PANEL] = y[:, at : at + PANEL] - dot_nn(y[:, 0:at], above)
 
         at = pl.multiple_of(p * PANEL, PANEL)
         panel_ref[...] = work[pl.ds(at, PANEL), pl.ds(at, PANEL)]
@@ -487,24 +503,18 @@
                 own = inv[at : at + PANEL, :]
                 if at + PANEL < order:
                     work[at : at + PANEL, at + PANEL :] = dot_nn(own, work[at : at + PANEL, at + PANEL :])
-                if y is not None:
-                    y[:, at : at + PANEL] = dot_nt(y[:, at : at + PANEL], own)
 
         return carry
 
     lax.fori_loop(0, count, panel, 0)
 
 
-def forward(work, inv, block, y, q):
+def forward(work, inv, block, q):
     at = q * PANEL
-    own = inv[at : at + PANEL, :]
-    value, vector = block[at : at + PANEL, :], y[:, at : at + PANEL]
+    value = block[at : at + PANEL, :]
     if q > 0:
-        above = work[0:at, at : at + PANEL]
-        value = value - dot_tn(above, block[0:at, :])
-        vector = vector - dot_nn(y[:, 0:at], above)
-    block[at : at + PANEL, :] = dot_nn(own, value)
-    y[:, at : at + PANEL] = dot_nt(vector, own)
+        value = value - dot_tn(work[0:at, at : at + PANEL], block[0:at, :])
+    block[at : at + PANEL, :] = dot_nn(inv[at : at + PANEL, :], value)
 
 
 def step_kernel(
@@ -530,7 +540,9 @@
     reg_ref,
     scaled_r,
     scaled_g,
-    reduced,
+    left_ref,
+    right_ref,
+    solved_ref,
     work,
     inv,
     block,
@@ -551,13 +563,13 @@
     regional_width, global_width = rprior_ref.shape[1], global_ref.shape[1]
     columns = regional_width + global_width
     rt, gt = regional_width // PANEL, global_width // PANEL
-    names = "01ABUVLMG"
+    names = "01ABUVLMHN"
     sections = {}
     for i, name in enumerate(names):
-        held = pieces[7 * i : 7 * i + 7]
+        held = pieces[5 * i : 5 * i + 5]
         sections[name] = Section(wide_plan if name == "0" else plan, *held[:3], held[3:])
-    pieces = pieces[7 * len(names) :]
-    joins = [Join(plan, n_regime, *pieces[7 * i : 7 * i + 3], pieces[7 * i + 3 : 7 * i + 7]) for i in range(gt)]
+    pieces = pieces[5 * len(names) :]
+    joins = [Join(plan, n_regime, *pieces[7 * i : 7 * i + 3], pieces[7 * i + 3 : 7 * i + 7]) for i in range(gt + 1)]
     staged = rt == 4 and gt == 4 and [radix for radix, _ in plan] == [2, 2, 4]
     places = schedule(sections, staged)
 
@@ -594,48 +606,52 @@
     for copy in share(scalars, 0):
         copy.start()
 
-    shape = (regional_width, width)
-    ids = lax.broadcasted_iota(jnp.int32, shape, 0)
-    regional = jnp.zeros(shape, F32)
     taps = tap_ref[...].astype(F32)
-    for k in range(index_ref.shape[0]):
-        regional = regional + jnp.where(
-            jnp.broadcast_to(index_ref[k : k + 1, :], shape) == ids,
-            jnp.broadcast_to(taps[k : k + 1, :], shape),
-            F32(0.0),
-        )
-    regional = regional.astype(BF16)
-    reg_ref[...] = regional
-    scaled_r[...] = (regional.astype(F32) * weight).astype(BF16)
     three = jnp.concatenate(split3(weighted), axis=0).astype(BF16)
     held = nparams * objects
     res3 = three_rows(residual, width)
+
+    def regional_rows(start, end):
+        shape = (end - start, width)
+        ids = lax.broadcasted_iota(jnp.int32, shape, 0) + start
+        regional = jnp.zeros(shape, F32)
+        for k in range(index_ref.shape[0]):
+            regional = regional + jnp.where(
+                jnp.broadcast_to(index_ref[k : k + 1, :], shape) == ids,
+                jnp.broadcast_to(taps[k : k + 1, :], shape),
+                F32(0.0),
+            )
+        regional = regional.astype(BF16)
+        reg_ref[start:end, :] = regional
+        scaled_r[start:end, :] = (regional.astype(F32) * weight).astype(BF16)
+        gradient = jnp.sum(dot_nt(res3, scaled_r[start:end, :], None), axis=0, keepdims=True)
+        return reduce_columns(dot_nt(three, reg_ref[start:end, :], None), gradient, start)
 
     def reduce_columns(product, gradient, offset):
         coupling = product[0:held] + product[held : 2 * held] + product[2 * held : 3 * held]
         lines = []
         for at in range(0, coupling.shape[1], PANEL):
             cols = slice(at, at + PANEL)
+            target = slice(offset + at, offset + at + PANEL)
             result = forward_small(factor, [coupling[a * objects : (a + 1) * objects, cols] for a in range(nparams)])
             dropped = vector[0] * result[0]
             for a in range(1, nparams):
                 dropped = dropped + vector[a] * result[a]
+            pieces = split3(jnp.concatenate(result, axis=0))
+            left_ref[:, target] = jnp.concatenate([pieces[t] for t in (0, 0, 1, 0, 1, 2)], axis=0).astype(BF16)
+            right_ref[:, target] = jnp.concatenate([pieces[t] for t in (0, 1, 0, 2, 1, 0)], axis=0).astype(BF16)
+            result = backward_small(factor, result)
             for a in range(nparams):
-                reduced[a * objects : (a + 1) * objects, offset + at : offset + at + PANEL] = result[a]
+                solved_ref[a * objects : (a + 1) * objects, target] = result[a]
             lines.append(gradient[:, cols] - jnp.sum(dropped, axis=0, keepdims=True))
-        pieces = split3(reduced[:, offset : offset + coupling.shape[1]])
-        left = jnp.concatenate([pieces[t] for t in (0, 0, 1, 0, 1, 2)], axis=0).astype(BF16)
-        right = jnp.concatenate([pieces[t] for t in (0, 1, 0, 2, 1, 0)], axis=0).astype(BF16)
-        return lines, left, right
-
-    gradient = jnp.sum(dot_nt(res3, scaled_r[...], None), axis=0, keepdims=True)
-    lines_r, left_r, right_r = reduce_columns(dot_nt(three, reg_ref[...], None), gradient, 0)
+        return lines
 
     def regional_line(i, start, end):
         own, rest = slice(i * PANEL, (i + 1) * PANEL), slice(start * PANEL, end * PANEL)
         line = dot_nt(scaled_r[own, :], reg_ref[rest, :], None) + dot_nt(reg_ref[own, :], scaled_r[rest, :], None)
-        return 0.5 * line - dot_tn(left_r[:, own], right_r[:, rest], None)
-
+        return 0.5 * line - dot_tn(left_ref[:, own], right_ref[:, rest], None)
+
+    lines_r = regional_rows(0, PANEL)
     corner = sections["0"]
     corner.part[0:PANEL, :] = regional_line(0, 0, 1)
     for copy in share(scalars, 0):
@@ -649,6 +665,7 @@
         lane == 0, both[0:1, :], jnp.where(lane == 1, both[1:2, :], corner.part[last:PANEL, :])
     )
     begin("0", PANEL)
+    lines_r = lines_r + regional_rows(PANEL, regional_width)
     begin("1", line_of_tiles(sections["1"].part, 0, regional_line(0, 1, rt)))
     begin("A", line_of_tiles(sections["A"].part, 0, regional_line(1, 1, rt)))
     at = 0
@@ -663,16 +680,17 @@
     column = jnp.transpose(eight)[:width, 0:1]
     scaled_g[...] = (global_ref[...].astype(F32) * column).astype(BF16)
     gradient = jnp.sum(dot_nn(res3, scaled_g[...], None), axis=0, keepdims=True)
-    lines_g, left_g, right_g = reduce_columns(dot_nn(three, global_ref[...], None), gradient, regional_width)
+    lines_g = reduce_columns(dot_nn(three, global_ref[...], None), gradient, regional_width)
 
     def mixed_line(i):
         own = slice(i * PANEL, (i + 1) * PANEL)
-        return dot_nn(scaled_r[own, :], global_ref[...], None) - dot_tn(left_r[:, own], right_g, None)
+        return dot_nn(scaled_r[own, :], global_ref[...], None) - dot_tn(left_ref[:, own], right_ref[:, regional_width:], None)
 
     def global_line(i):
         own, rest = slice(i * PANEL, (i + 1) * PANEL), slice(i * PANEL, global_width)
         line = dot_tn(scaled_g[:, own], global_ref[:, rest], None) + dot_tn(global_ref[:, own], scaled_g[:, rest], None)
-        return 0.5 * line - dot_tn(left_g[:, own], right_g[:, rest], None)
+        own, rest = (slice(regional_width + x.start, regional_width + x.stop) for x in (own, rest))
+        return 0.5 * line - dot_tn(left_ref[:, own], right_ref[:, rest], None)
 
     progress("C4a")
     rhs_at = line_of_tiles(sections["U"].part, 0, mixed_line(0))
@@ -688,11 +706,13 @@
     for i in range(3, rt):
         at = line_of_tiles(sections["M"].part, at, mixed_line(i))
     begin("M", at)
-    progress("C6")
+    progress("C6a")
+    begin("H", line_of_tiles(sections["H"].part, 0, global_line(0)))
+    progress("C6b")
     at = 0
-    for i in range(gt):
-        at = line_of_tiles(sections["G"].part, at, global_line(i))
-    begin("G", at)
+    for i in range(1, gt):
+        at = line_of_tiles(sections["N"].part, at, global_line(i))
+    begin("N", at)
     progress("upd0")
 
     sums = corner.result()[last:PANEL, :]
@@ -738,7 +758,7 @@
         if q == 0:
             unpack_row("1", 0, 1)
 
-    eliminate(work, inv, None, before, after, panel_ref, spread_ref, pause)
+    eliminate(work, inv, before, after, panel_ref, spread_ref, pause)
     for i in range(rt):
         progress(f"X{i}")
         name, at = ("UVL"[i], 0) if i < 3 else ("M", (i - 3) * gt * PANEL)
@@ -746,37 +766,42 @@
         for j in range(gt):
             block[own, j * PANEL : (j + 1) * PANEL] = sections[name].result()[at : at + PANEL, :]
             at += PANEL
-        if i == 0:
-            rhs = sections["U"].result()
-            for c in range(rt):
-                y[:, c * PANEL : (c + 1) * PANEL] = jnp.broadcast_to(rhs[rhs_at + c : rhs_at + c + 1, :], tile)
-        forward(work, inv, block, y, i)
+        forward(work, inv, block, i)
+        forward_vector(work, inv, y, sections["U"].result()[rhs_at + i : rhs_at + i + 1, :], i)
     rhs = sections["U"].result()
-    dropped = dot_nn(y[...], block[...])
+    dropped = times_column(block[...], y[...])
     vectors[0] = jnp.zeros(tile, F32)
     for j in range(gt):
         at = rhs_at + rt + j
-        vectors[0, j : j + 1, :] = rhs[at : at + 1, :] - dropped[0:1, j * PANEL : (j + 1) * PANEL]
+        vectors[0, j : j + 1, :] = rhs[at : at + 1, :] - dropped[:, j * PANEL : (j + 1) * PANEL]
     for copy in share(vectors, 1):
         copy.start()
-    for i in range(gt):
-        line = dot_tn(block[:, i * PANEL : (i + 1) * PANEL], block[:, i * PANEL :])
-        line_of_tiles(joins[i].part, 0, line)
-    progress("join")
+
+    def join_line(join, i, start, end, name, at):
+        own, rest = slice(i * PANEL, (i + 1) * PANEL), slice(start * PANEL, end * PANEL)
+        line = dot_tn(block[:, own], block[:, rest])
+        progress({"H": "J0", "N": "J1"}[name] if (i, start) in ((0, 0), (1, 1)) else None)
+        for j in range(end - start):
+            join.part[j * PANEL : (j + 1) * PANEL, :] = (
+                sections[name].result()[at : at + PANEL, :] - line[:, j * PANEL : (j + 1) * PANEL]
+            )
+            at += PANEL
+        join.start()
+        return at
+
+    at = join_line(joins[0], 0, 0, 1, "H", 0)
+    join_line(joins[1], 0, 1, gt, "H", at)
     at = 0
-    for i in range(gt):
-        size = joins[i].part.shape[0]
-        joins[i].part[...] = sections["G"].result()[at : at + size, :] - joins[i].part[...]
-        at += size
-        joins[i].start()
-
-    def unpack(i):
-        for j in range(i, gt):
-            gwork[i * PANEL : (i + 1) * PANEL, j * PANEL : (j + 1) * PANEL] = joins[i].full[
-                (j - i) * PANEL : (j - i + 1) * PANEL, :
+    for i in range(1, gt):
+        at = join_line(joins[i + 1], i, i, gt, "N", at)
+    joins[0].add()
+
+    def unpack(join, i, start, end):
+        for j in range(start, end):
+            gwork[i * PANEL : (i + 1) * PANEL, j * PANEL : (j + 1) * PANEL] = join.full[
+                (j - start) * PANEL : (j - start + 1) * PANEL, :
             ]
 
-    joins[0].add()
     for copy in share(vectors, 1):
         copy.wait()
     vector_sum = None
@@ -785,39 +810,37 @@
         for k in range(n_regime - 1):
             line = jnp.where(lax.rem(r + n_regime - k - 1, n_regime) == g, vectors[k + 1], line)
         vector_sum = line if vector_sum is None else vector_sum + line
-    for j in range(gt):
-        gy[:, j * PANEL : (j + 1) * PANEL] = jnp.broadcast_to(vector_sum[j : j + 1, :], tile)
     joins[0].finish()
 
     def before_global(q):
-        if q > 0:
-            joins[q].finish()
-        unpack(q)
+        if q == 0:
+            unpack(joins[0], 0, 0, 1)
+        else:
+            joins[q + 1].finish()
+            unpack(joins[q + 1], q, q, gt)
         diagonal(gwork, gprior_ref, q)
 
     def after_global(q):
         if q == 0:
             for join in joins[1:]:
                 join.add()
-
-    eliminate(gwork, ginv, gy, before_global, after_global, panel_ref, spread_ref)
-    back_substitute(gwork, ginv, gy)
-    global_step[...] = gy[0:1, :]
-    y[...] = y[...] - dot_nt(gy[...], block[...])
-    back_substitute(work, inv, y)
-    regional_step[...] = y[0:1, :]
-
-    moved = dot_nn(three_rows(y[0:1, :], regional_width), reg_ref[...], None)
-    moved = moved + dot_nt(three_rows(gy[0:1, :], global_width), global_ref[...], None)
-    moved = jnp.sum(moved, axis=0, keepdims=True)
-    target = jnp.sum(weighted * (residual - moved), axis=1, keepdims=True)
+            joins[1].finish()
+            unpack(joins[1], 0, 1, gt)
+        forward_vector(gwork, ginv, gy, vector_sum[q : q + 1, :], q)
+
+    eliminate(gwork, ginv, before_global, after_global, panel_ref, spread_ref)
+    back_substitute(gwork, ginv, gy, global_step)
+    y[...] = y[...] - times_row(block[...], global_step[...])
+    back_substitute(work, inv, y, regional_step)
+
+    moved = times_row(solved_ref[:, regional_width:], global_step[...])
+    moved = moved + times_row(solved_ref[:, 0:regional_width], regional_step[...])
     vreg = (objects, PANEL)
-    targets = [jnp.broadcast_to(target[a * objects : (a + 1) * objects, :], vreg) for a in range(nparams)]
-    solved = backward_small(factor, forward_small(factor, targets))
     lane = lax.broadcasted_iota(jnp.int32, vreg, 1)
+    steady = backward_small(factor, vector)
     side = jnp.zeros(vreg, F32)
     for a in range(nparams):
-        side = jnp.where(lane == a, solved[a], side)
+        side = jnp.where(lane == a, steady[a] - moved[a * objects : (a + 1) * objects, :], side)
     local_step[...] = jnp.transpose(side)[0:nparams, 0:objects]
 
 
@@ -863,7 +886,8 @@
         gt,
         gt,
         (rt - 3) * gt,
-        gt * (gt + 1) // 2,
+        gt,
+        gt * (gt - 1) // 2,
     ]
     sections = [tiles * PANEL for tiles in sections]
     sections[4] += columns // PANEL
@@ -874,14 +898,16 @@
         buffer(regional_width, width, dtype=BF16),
         buffer(regional_width, width, dtype=BF16),
         buffer(width, order, dtype=BF16),
+        buffer(6 * nparams * objects, columns, dtype=BF16),
+        buffer(6 * nparams * objects, columns, dtype=BF16),
         buffer(nparams * objects, columns),
         buffer(regional_width, regional_width),
         buffer(regional_width, PANEL),
         buffer(regional_width, order),
-        buffer(GROUP, regional_width),
+        buffer(regional_width, PANEL),
         buffer(order, order),
         buffer(order, PANEL),
-        buffer(GROUP, order),
+        buffer(order, PANEL),
         buffer(n_regime, GROUP, PANEL),
         buffer(n_regime, GROUP, PANEL),
         pltpu.SemaphoreType.DMA((2, peers)),
@@ -889,8 +915,8 @@
     ]
     for i, rows in enumerate(sections):
         scratch += section_scratch(padded(rows, n_obj), plan if i else wide_plan)
-    for i in range(gt):
-        scratch += join_scratch((gt - i) * PANEL, plan, n_regime)
+    for tiles in [1] + list(range(gt - 1, 0, -1))[:1] + list(range(gt - 1, 0, -1)):
+        scratch += join_scratch(tiles * PANEL, plan, n_regime)
     shapes = ((nparams, objects), (1, regional_width), (1, order))
     local_step, regional_step, global_step = pl.pallas_call(
         functools.partial(step_kernel, plan, wide_plan, n_regime),

time: 82.7 us -> 71.7 us (0.87)
  Pallas kernels: 79.2 us -> 68.2 us
    pallas_call x1, Pallas kernels: 79.2 us -> 68.2 us  [body(): pl.pallas_call(functools.partial(step_kernel, plan, wide_plan, n_regime),...]
where the time goes in v4:
time: 71.7 us; the launch traced here: 71.5 us
  Pallas kernels  68.2 us (95%)
  local copies, waits for them, and re-layouts  2.59 us (4%)
    pallas_call x1, Pallas kernels, body(): pl.pallas_call(functools.partial(step_kernel, plan, wide_plan, n_regime),...  68.2 us
    unnamed x9, local copies, waits for them, and re-layouts  2.59 us

profile of v4, /device:TPU:0, one launch (start us, length us, event | category | flops | bytes accessed | tf_op | source)
XLA Modules:
  0.0 71.5 jit_solution(8044571541413157594)
XLA Ops:
  0.6 68.2 %step.1 = (f32[7,8]{1,0:T(8,128)}, f32[1,512]{1,0:T(1,128)}, f32[1,512]{1,0:T(1,128)}) custom-call(s32[8]{0:T(128)} %count_ref.1, f32[7,8]{1,0:T(8,128)} %prior_ref.1, bf16[7,480]{1,0:T(8,128)(2,1)} %local_ref.1, bf16[480,512]{1,0:T(8,128)(2,1)} %global_ref.1, s32[4,480]{1,0:T(4,128)} %index_ref.1, bf16[4,480]{1,0:T(4,128)(2,1)} %tap_ref.1, ...), custom_call_target="tpu_custom_call" | custom-call | tf_op jit(solution)/shard_map/step/pallas_call | solution.py:921
  68.9 0.0 copy-start
  68.9 0.7 copy-done
  69.5 0.0 copy-start.2
  69.5 0.6 copy.16
  70.1 0.1 copy-done.2
  70.2 0.0 copy-start.1
  70.2 0.6 copy.17
  70.8 0.1 copy-done.1
  70.9 0.6 copy.18
Async XLA Ops:
  68.9 0.7 copy-start
  69.5 0.7 copy-start.2
  70.2 0.7 copy-start.1

commit v5 on v4

--- a/solution.py
+++ b/solution.py
@@ -306,16 +306,18 @@
     return jnp.where(sub == 0, high, jnp.where(sub == 1, middle, jnp.where(sub == 2, low, zero))).astype(BF16)
 
 
-def local_pieces(local_ref, residual_ref, obs_ref, count_ref, prior_ref, rows8):
+def local_pieces(local_ref, residual_ref, obs_ref, count_ref, prior_ref, rows8, side_ref):
     nparams, width = local_ref.shape
-    objects = count_ref.shape[0]
+    objects = count_ref.shape[1]
     observed = width // objects
     shape = (objects, width)
     lane = lax.broadcasted_iota(jnp.int32, shape, 1)
     sub = lax.broadcasted_iota(jnp.int32, shape, 0)
-    counts = jnp.zeros(shape, jnp.int32)
-    for n in range(objects):
-        counts = jnp.where(sub == n, count_ref[n], counts)
+    side_ref[...] = jnp.zeros(side_ref.shape, F32)
+    side_ref[0:nparams, 0:objects] = prior_ref[...]
+    side_ref[nparams : nparams + 1, 0:objects] = count_ref[...].astype(F32)
+    turned = jnp.transpose(side_ref[...])[0:objects, :]
+    counts = jnp.broadcast_to(turned[:, nparams : nparams + 1], shape).astype(jnp.int32)
     position = lane - sub * observed
     present = (position >= 0) & (position < counts)
     weights = jnp.where(present, jnp.broadcast_to(obs_ref[...], shape), F32(0.0))
@@ -330,16 +332,12 @@
     )
     small = dot_nt(weighted, rows8[...])
     vreg = (objects, PANEL)
-    row = lax.broadcasted_iota(jnp.int32, vreg, 0)
 
     def entry(a, b):
         return jnp.broadcast_to(small[a * objects : (a + 1) * objects, b : b + 1], vreg)
 
     def prior(a):
-        value = jnp.zeros(vreg, F32)
-        for n in range(objects):
-            value = jnp.where(row == n, prior_ref[a, n], value)
-        return value
+        return jnp.broadcast_to(turned[:, a : a + 1], vreg)
 
     entries = [
         [entry(a, b) + prior(a) if a == b else (entry(a, b) if a > b else None) for b in range(nparams)]
@@ -521,19 +519,35 @@
     plan,
     wide_plan,
     n_regime,
+    *refs,
+):
+    given, packed, held, refs = refs[0:10], refs[10], refs[11:21], refs[21:]
+    arrive = refs[0]
+    arrivals = [pltpu.make_async_copy(src, dst, arrive.at[i]) for i, (src, dst) in enumerate(zip(given, held))]
+    for copy in arrivals:
+        copy.start()
+    inner_kernel(plan, wide_plan, n_regime, arrivals, *held, packed, *refs[1:])
+
+
+def inner_kernel(
+    plan,
+    wide_plan,
+    n_regime,
+    arrivals,
     count_ref,
     prior_ref,
     local_ref,
-    global_ref,
+    residual_ref,
+    obs_ref,
     index_ref,
     tap_ref,
-    residual_ref,
-    obs_ref,
+    global_ref,
     rprior_ref,
     gprior_ref,
-    local_step,
+    packed,
     regional_step,
     global_step,
+    side_ref,
     rows8,
     panel_ref,
     spread_ref,
@@ -559,7 +573,7 @@
     barrier, total = enter(wide_plan, n_regime)
     r, o = lax.axis_index("regime"), lax.axis_index("obj")
     nparams, width = local_ref.shape
-    objects = count_ref.shape[0]
+    objects = count_ref.shape[1]
     regional_width, global_width = rprior_ref.shape[1], global_ref.shape[1]
     columns = regional_width + global_width
     rt, gt = regional_width // PANEL, global_width // PANEL
@@ -597,8 +611,10 @@
             for k in range(n_regime - 1)
         ]
 
+    for copy in arrivals[0:5]:
+        copy.wait()
     weight, residual, misfit, counted, weighted, factor, vector = local_pieces(
-        local_ref, residual_ref, obs_ref, count_ref, prior_ref, rows8
+        local_ref, residual_ref, obs_ref, count_ref, prior_ref, rows8, side_ref
     )
     sub = lax.broadcasted_iota(jnp.int32, tile, 0)
     scalars[0] = jnp.where(sub == 0, misfit, jnp.where(sub == 1, counted, F32(0.0)))
@@ -606,6 +622,8 @@
     for copy in share(scalars, 0):
         copy.start()
 
+    for copy in arrivals[5:7]:
+        copy.wait()
     taps = tap_ref[...].astype(F32)
     three = jnp.concatenate(split3(weighted), axis=0).astype(BF16)
     held = nparams * objects
@@ -673,6 +691,8 @@
         at = line_of_tiles(sections["B"].part, at, regional_line(i, i, rt))
     begin("B", at)
 
+    for copy in arrivals[7:]:
+        copy.wait()
     wide = -(-width // PANEL) * PANEL
     eight = jnp.broadcast_to(weight, (GROUP, width))
     if wide > width:
@@ -822,13 +842,20 @@
 
     def after_global(q):
         if q == 0:
-            for join in joins[1:]:
-                join.add()
             joins[1].finish()
             unpack(joins[1], 0, 1, gt)
         forward_vector(gwork, ginv, gy, vector_sum[q : q + 1, :], q)
 
-    eliminate(gwork, ginv, before_global, after_global, panel_ref, spread_ref)
+    def pause_global(p, g):
+        quarter = PANEL // GROUP // 4
+        if (g + 1) % quarter or (g + 1) // quarter not in (2, 3):
+            return
+        for q in range(gt):
+            which = 1 if q == 0 and (g + 1) // quarter == 2 else q + 2
+            if ((g + 1) // quarter == 3 or q == 0) and which <= gt:
+                pl.when(p == q)(joins[which].add)
+
+    eliminate(gwork, ginv, before_global, after_global, panel_ref, spread_ref, pause_global)
     back_substitute(gwork, ginv, gy, global_step)
     y[...] = y[...] - times_row(block[...], global_step[...])
     back_substitute(work, inv, y, regional_step)
@@ -841,15 +868,19 @@
     side = jnp.zeros(vreg, F32)
     for a in range(nparams):
         side = jnp.where(lane == a, steady[a] - moved[a * objects : (a + 1) * objects, :], side)
-    local_step[...] = jnp.transpose(side)[0:nparams, 0:objects]
+    packed[0:GROUP, 0:objects] = jnp.transpose(side)[0:GROUP, 0:objects]
+    packed[GROUP : GROUP + 1, 0:regional_width] = regional_step[...]
+    packed[GROUP + 1 : GROUP + 2, 0:global_width] = global_step[...]
+
+
+def deliver_kernel(packed, local_step, regional_step, global_step):
+    local_step[...] = packed[0 : local_step.shape[0], 0 : local_step.shape[1]]
+    regional_step[...] = packed[GROUP : GROUP + 1, 0 : regional_step.shape[1]]
+    global_step[...] = packed[GROUP + 1 : GROUP + 2, 0 : global_step.shape[1]]
 
 
 def vmem(count):
     return [pl.BlockSpec(memory_space=pltpu.VMEM)] * count
-
-
-def smem(count):
-    return [pl.BlockSpec(memory_space=pltpu.SMEM)] * count
 
 
 def body(
@@ -891,7 +922,24 @@
     ]
     sections = [tiles * PANEL for tiles in sections]
     sections[4] += columns // PANEL
-    scratch = [
+    inputs = (
+        obs_count[None, :],
+        local_prior,
+        local_jac,
+        residual[None, :],
+        obs_weight[None, :],
+        coeff_index,
+        coeff_weight,
+        global_jac,
+        regional_prior,
+        global_prior[None, :],
+    )
+    scratch = [buffer(*x.shape, dtype=x.dtype) for x in inputs]
+    scratch += [
+        pltpu.SemaphoreType.DMA((len(inputs),)),
+        buffer(1, regional_width),
+        buffer(1, order),
+        buffer(GROUP, PANEL),
         buffer(nparams + 1, width),
         buffer(PANEL, PANEL),
         buffer(GROUP * GROUP, PANEL),
@@ -918,26 +966,22 @@
     for tiles in [1] + list(range(gt - 1, 0, -1))[:1] + list(range(gt - 1, 0, -1)):
         scratch += join_scratch(tiles * PANEL, plan, n_regime)
     shapes = ((nparams, objects), (1, regional_width), (1, order))
-    local_step, regional_step, global_step = pl.pallas_call(
+    packed = pl.pallas_call(
         functools.partial(step_kernel, plan, wide_plan, n_regime),
-        out_shape=tuple(jax.ShapeDtypeStruct(shape, F32) for shape in shapes),
-        in_specs=smem(2) + vmem(8),
-        out_specs=tuple(vmem(3)),
+        out_shape=jax.ShapeDtypeStruct((2 * GROUP, max(regional_width, order)), F32),
+        in_specs=[pl.BlockSpec(memory_space=pl.ANY)] * len(inputs),
+        out_specs=vmem(1)[0],
         scratch_shapes=scratch,
         compiler_params=pltpu.CompilerParams(collective_id=0, has_side_effects=True),
         name="step",
-    )(
-        obs_count,
-        local_prior,
-        local_jac,
-        global_jac,
-        coeff_index,
-        coeff_weight,
-        residual[None, :],
-        obs_weight[None, :],
-        regional_prior,
-        global_prior[None, :],
-    )
+    )(*inputs)
+    local_step, regional_step, global_step = pl.pallas_call(
+        deliver_kernel,
+        out_shape=tuple(jax.ShapeDtypeStruct(shape, F32) for shape in shapes),
+        in_specs=vmem(1),
+        out_specs=tuple(vmem(3)),
+        name="deliver",
+    )(packed)
     return (local_step, regional_step, global_step[0])
 
 

time: 71.7 us -> 69.6 us (0.971)
  local copies, waits for them, and re-layouts: 2.59 us -> 0 us
    unnamed x9 -> x0, local copies, waits for them, and re-layouts: 2.59 us -> none
    pallas_call x0 -> x1, Pallas kernels: none -> 1.36 us  [body(): pl.pallas_call(deliver_kernel, out_shape=tuple((jax.ShapeDtypeStruct(shap...]
    pallas_call x1, Pallas kernels: 68.2 us -> 67.4 us  [body(): pl.pallas_call(functools.partial(step_kernel, plan, wide_plan, n_regime),...]
where the time goes in v5:
time: 69.6 us; the launch traced here: 69.4 us
  Pallas kernels  68.7 us (99%)
    pallas_call x1, Pallas kernels, body(): pl.pallas_call(functools.partial(step_kernel, plan, wide_plan, n_regime),...  67.4 us

profile of v5, /device:TPU:0, one launch (start us, length us, event | category | flops | bytes accessed | tf_op | source)
XLA Modules:
  0.0 69.4 jit_solution(5772318302374429450)
XLA Ops:
  0.6 67.4 %step.1.packed = f32[16,512]{1,0:T(8,128)} custom-call(s32[1,8]{1,0:T(1,128)} %bitcast.8, f32[7,8]{1,0:T(8,128)} %refs_1_.1, bf16[7,480]{1,0:T(8,128)(2,1)} %refs_2_.1, f32[1,480]{1,0:T(1,128)} %bitcast.5, f32[1,480]{1,0:T(1,128)} %bitcast.6, s32[4,480]{1,0:T(4,128)} %refs_5_.1, bf16[4,480]{1,0:T(4,128)(2,1)} %refs_6_.1, bf16[480,512]{1,0:T(8,128)(2,1)} %refs_7_.1, ...), custom_call_target="tpu_custom_call" | custom-call | tf_op jit(solution)/shard_map/step/pallas_call | solution.py:969
  68.0 1.4 %deliver.1 = (f32[7,8]{1,0:T(8,128)}, f32[1,512]{1,0:T(1,128)}, f32[1,512]{1,0:T(1,128)}) custom-call(f32[16,512]{1,0:T(8,128)} %step.1.packed), custom_call_target="tpu_custom_call" | custom-call | tf_op jit(solution)/shard_map/deliver/pallas_call | solution.py:978

commit v6 on v5

--- a/solution.py
+++ b/solution.py
@@ -164,7 +164,8 @@
     "inv3.3": "H",
     "X1": "MLNV",
     "X3": "HM",
-    "J0": "NH",
+    "J0": "H",
+    "J0b": "N",
     "J1": "N",
 }
 
@@ -473,7 +474,7 @@
         x[:, own] = times_column(inv[own, :], current)
 
 
-def eliminate(work, inv, before, after, panel_ref, spread_ref, pause=None):
+def eliminate(work, inv, before, after, panel_ref, spread_ref, pause=None, late=None):
     order = work.shape[0]
     count = order // PANEL
 
@@ -486,7 +487,8 @@
                 at = q * PANEL
                 if q > 0:
                     above = work[0:at, at : at + PANEL]
-                    work[at : at + PANEL, at:] = work[at : at + PANEL, at:] - dot_tn(above, work[0:at, at:])
+                    end = at + PANEL if q == late else order
+                    work[at : at + PANEL, at:end] = work[at : at + PANEL, at:end] - dot_tn(above, work[0:at, at:end])
 
         at = pl.multiple_of(p * PANEL, PANEL)
         panel_ref[...] = work[pl.ds(at, PANEL), pl.ds(at, PANEL)]
@@ -500,7 +502,10 @@
                 at = q * PANEL
                 own = inv[at : at + PANEL, :]
                 if at + PANEL < order:
-                    work[at : at + PANEL, at + PANEL :] = dot_nn(own, work[at : at + PANEL, at + PANEL :])
+                    rest = work[at : at + PANEL, at + PANEL :]
+                    if q == late:
+                        rest = rest - dot_tn(work[0:at, at : at + PANEL], work[0:at, at + PANEL :])
+                    work[at : at + PANEL, at + PANEL :] = dot_nn(own, rest)
 
         return carry
 
@@ -583,7 +588,7 @@
         held = pieces[5 * i : 5 * i + 5]
         sections[name] = Section(wide_plan if name == "0" else plan, *held[:3], held[3:])
     pieces = pieces[5 * len(names) :]
-    joins = [Join(plan, n_regime, *pieces[7 * i : 7 * i + 3], pieces[7 * i + 3 : 7 * i + 7]) for i in range(gt + 1)]
+    joins = [Join(plan, n_regime, *pieces[7 * i : 7 * i + 3], pieces[7 * i + 3 : 7 * i + 7]) for i in range(gt + 2)]
     staged = rt == 4 and gt == 4 and [radix for radix, _ in plan] == [2, 2, 4]
     places = schedule(sections, staged)
 
@@ -789,6 +794,23 @@
         forward(work, inv, block, i)
         forward_vector(work, inv, y, sections["U"].result()[rhs_at + i : rhs_at + i + 1, :], i)
     rhs = sections["U"].result()
+
+    def join_line(join, i, start, end, name, at):
+        own, rest = slice(i * PANEL, (i + 1) * PANEL), slice(start * PANEL, end * PANEL)
+        if (i, start) == (0, 1):
+            progress("J0b")
+        line = dot_tn(block[:, own], block[:, rest])
+        progress({(0, 0): "J0", (1, 1): "J1"}.get((i, start)))
+        for j in range(end - start):
+            join.part[j * PANEL : (j + 1) * PANEL, :] = (
+                sections[name].result()[at : at + PANEL, :] - line[:, j * PANEL : (j + 1) * PANEL]
+            )
+            at += PANEL
+        join.start()
+        return at
+
+    at = join_line(joins[0], 0, 0, 1, "H", 0)
+    join_line(joins[1], 0, 1, gt, "H", at)
     dropped = times_column(block[...], y[...])
     vectors[0] = jnp.zeros(tile, F32)
     for j in range(gt):
@@ -796,24 +818,10 @@
         vectors[0, j : j + 1, :] = rhs[at : at + 1, :] - dropped[:, j * PANEL : (j + 1) * PANEL]
     for copy in share(vectors, 1):
         copy.start()
-
-    def join_line(join, i, start, end, name, at):
-        own, rest = slice(i * PANEL, (i + 1) * PANEL), slice(start * PANEL, end * PANEL)
-        line = dot_tn(block[:, own], block[:, rest])
-        progress({"H": "J0", "N": "J1"}[name] if (i, start) in ((0, 0), (1, 1)) else None)
-        for j in range(end - start):
-            join.part[j * PANEL : (j + 1) * PANEL, :] = (
-                sections[name].result()[at : at + PANEL, :] - line[:, j * PANEL : (j + 1) * PANEL]
-            )
-            at += PANEL
-        join.start()
-        return at
-
-    at = join_line(joins[0], 0, 0, 1, "H", 0)
-    join_line(joins[1], 0, 1, gt, "H", at)
-    at = 0
-    for i in range(1, gt):
-        at = join_line(joins[i + 1], i, i, gt, "N", at)
+    at = join_line(joins[2], 1, 1, 2, "N", 0)
+    at = join_line(joins[3], 1, 2, gt, "N", at)
+    for i in range(2, gt):
+        at = join_line(joins[i + 2], i, i, gt, "N", at)
     joins[0].add()
 
     def unpack(join, i, start, end):
@@ -822,40 +830,52 @@
                 (j - start) * PANEL : (j - start + 1) * PANEL, :
             ]
 
-    for copy in share(vectors, 1):
-        copy.wait()
-    vector_sum = None
-    for g in range(n_regime):
-        line = vectors[0]
-        for k in range(n_regime - 1):
-            line = jnp.where(lax.rem(r + n_regime - k - 1, n_regime) == g, vectors[k + 1], line)
-        vector_sum = line if vector_sum is None else vector_sum + line
     joins[0].finish()
+
+    def add_vectors():
+        for copy in share(vectors, 1):
+            copy.wait()
+        vector_sum = None
+        for g in range(n_regime):
+            line = vectors[0]
+            for k in range(n_regime - 1):
+                line = jnp.where(lax.rem(r + n_regime - k - 1, n_regime) == g, vectors[k + 1], line)
+            vector_sum = line if vector_sum is None else vector_sum + line
+        side_ref[...] = vector_sum
 
     def before_global(q):
         if q == 0:
             unpack(joins[0], 0, 0, 1)
+        elif q == 1:
+            joins[2].finish()
+            unpack(joins[2], 1, 1, 2)
         else:
-            joins[q + 1].finish()
-            unpack(joins[q + 1], q, q, gt)
+            joins[q + 2].finish()
+            unpack(joins[q + 2], q, q, gt)
         diagonal(gwork, gprior_ref, q)
 
     def after_global(q):
         if q == 0:
             joins[1].finish()
             unpack(joins[1], 0, 1, gt)
-        forward_vector(gwork, ginv, gy, vector_sum[q : q + 1, :], q)
+            add_vectors()
+        if q == 1:
+            joins[3].finish()
+            unpack(joins[3], 1, 2, gt)
+        forward_vector(gwork, ginv, gy, side_ref[q : q + 1, :], q)
 
     def pause_global(p, g):
         quarter = PANEL // GROUP // 4
-        if (g + 1) % quarter or (g + 1) // quarter not in (2, 3):
+        if (g + 1) % quarter:
             return
         for q in range(gt):
-            which = 1 if q == 0 and (g + 1) // quarter == 2 else q + 2
-            if ((g + 1) // quarter == 3 or q == 0) and which <= gt:
+            which = {(0, 2): 1, (0, 3): 2, (1, 2): 3}.get((q, (g + 1) // quarter))
+            if q > 0 and (g + 1) // quarter == 3 and q + 1 < gt:
+                which = q + 3
+            if which is not None:
                 pl.when(p == q)(joins[which].add)
 
-    eliminate(gwork, ginv, before_global, after_global, panel_ref, spread_ref, pause_global)
+    eliminate(gwork, ginv, before_global, after_global, panel_ref, spread_ref, pause_global, 1)
     back_substitute(gwork, ginv, gy, global_step)
     y[...] = y[...] - times_row(block[...], global_step[...])
     back_substitute(work, inv, y, regional_step)
@@ -963,7 +983,7 @@
     ]
     for i, rows in enumerate(sections):
         scratch += section_scratch(padded(rows, n_obj), plan if i else wide_plan)
-    for tiles in [1] + list(range(gt - 1, 0, -1))[:1] + list(range(gt - 1, 0, -1)):
+    for tiles in [1, gt - 1, 1, gt - 2] + list(range(gt - 2, 0, -1)):
         scratch += join_scratch(tiles * PANEL, plan, n_regime)
     shapes = ((nparams, objects), (1, regional_width), (1, order))
     packed = pl.pallas_call(

time: 69.6 us -> 69 us (level)
  no operation moved by 1% of the time
where the time goes in v6:
time: 69 us; the launch traced here: 68.8 us
  Pallas kernels  68.1 us (99%)
    pallas_call x1, Pallas kernels, body(): pl.pallas_call(functools.partial(step_kernel, plan, wide_plan, n_regime),...  66.8 us

profile of v6, /device:TPU:0, one launch (start us, length us, event | category | flops | bytes accessed | tf_op | source)
XLA Modules:
  0.0 68.8 jit_solution(1586734403741013722)
XLA Ops:
  0.6 66.8 %step.1.packed = f32[16,512]{1,0:T(8,128)} custom-call(s32[1,8]{1,0:T(1,128)} %bitcast.8, f32[7,8]{1,0:T(8,128)} %refs_1_.1, bf16[7,480]{1,0:T(8,128)(2,1)} %refs_2_.1, f32[1,480]{1,0:T(1,128)} %bitcast.5, f32[1,480]{1,0:T(1,128)} %bitcast.6, s32[4,480]{1,0:T(4,128)} %refs_5_.1, bf16[4,480]{1,0:T(4,128)(2,1)} %refs_6_.1, bf16[480,512]{1,0:T(8,128)(2,1)} %refs_7_.1, ...), custom_call_target="tpu_custom_call" | custom-call | tf_op jit(solution)/shard_map/step/pallas_call | solution.py:989
  67.4 1.4 %deliver.1 = (f32[7,8]{1,0:T(8,128)}, f32[1,512]{1,0:T(1,128)}, f32[1,512]{1,0:T(1,128)}) custom-call(f32[16,512]{1,0:T(8,128)} %step.1.packed), custom_call_target="tpu_custom_call" | custom-call | tf_op jit(solution)/shard_map/deliver/pallas_call | solution.py:998

commit v7 on v6

--- a/solution.py
+++ b/solution.py
@@ -106,7 +106,6 @@
 
     def copies(self, at):
         kind, stage, to, there, own, sub, used = self.steps[at]
-        first = sum(len(step[2]) for step in self.steps[:at])
         result = []
         for k, device in enumerate(to):
             if kind == "scatter":
@@ -118,8 +117,8 @@
                 pltpu.make_async_remote_copy(
                     src_ref=src,
                     dst_ref=dst,
-                    send_sem=self.sems[0].at[k],
-                    recv_sem=self.sems[1].at[first + k],
+                    send_sem=self.sems[0].at[0],
+                    recv_sem=self.sems[1].at[at],
                     device_id=device,
                     device_id_type=MESH,
                 )
@@ -131,9 +130,17 @@
             copy.start()
 
     def finish(self, at):
-        for copy in self.copies(at):
-            copy.wait()
         kind, stage, to, there, own, sub, used = self.steps[at]
+        size = len(to) * sub
+        place = self.recv.at[pl.ds(used, size)] if kind == "scatter" else self.full.at[pl.ds(0, size)]
+        pltpu.make_async_remote_copy(
+            src_ref=place,
+            dst_ref=place,
+            send_sem=self.sems[0].at[0],
+            recv_sem=self.sems[1].at[at],
+            device_id=to[0],
+            device_id_type=MESH,
+        ).wait()
         if kind == "scatter":
             rows = pl.ds(own, sub)
             total = self.part[rows, :]
@@ -235,10 +242,9 @@
 
 
 def section_scratch(rows, plan):
-    widths = [radix - 1 for radix, _ in plan] + [1]
     return [pltpu.VMEM((rows, PANEL), F32)] * 3 + [
-        pltpu.SemaphoreType.DMA((max(widths),)),
-        pltpu.SemaphoreType.DMA((2 * sum(widths[:-1]) or 1,)),
+        pltpu.SemaphoreType.DMA((1,)),
+        pltpu.SemaphoreType.DMA((2 * len(plan) or 1,)),
     ]
 
 

time: 69 us -> 68.3 us (0.990)
  no operation moved by 1% of the time
where the time goes in v7:
time: 68.3 us; the launch traced here: 68.1 us
  Pallas kernels  67.5 us (99%)
    pallas_call x1, Pallas kernels, body(): pl.pallas_call(functools.partial(step_kernel, plan, wide_plan, n_regime),...  66.1 us

profile of v7, /device:TPU:0, one launch (start us, length us, event | category | flops | bytes accessed | tf_op | source)
XLA Modules:
  0.0 68.1 jit_solution(592505682252449411)
XLA Ops:
  0.6 66.1 %step.1.packed = f32[16,512]{1,0:T(8,128)} custom-call(s32[1,8]{1,0:T(1,128)} %bitcast.8, f32[7,8]{1,0:T(8,128)} %refs_1_.1, bf16[7,480]{1,0:T(8,128)(2,1)} %refs_2_.1, f32[1,480]{1,0:T(1,128)} %bitcast.5, f32[1,480]{1,0:T(1,128)} %bitcast.6, s32[4,480]{1,0:T(4,128)} %refs_5_.1, bf16[4,480]{1,0:T(4,128)(2,1)} %refs_6_.1, bf16[480,512]{1,0:T(8,128)(2,1)} %refs_7_.1, ...), custom_call_target="tpu_custom_call" | custom-call | tf_op jit(solution)/shard_map/step/pallas_call | solution.py:995
  66.8 1.4 %deliver.1 = (f32[7,8]{1,0:T(8,128)}, f32[1,512]{1,0:T(1,128)}, f32[1,512]{1,0:T(1,128)}) custom-call(f32[16,512]{1,0:T(8,128)} %step.1.packed), custom_call_target="tpu_custom_call" | custom-call | tf_op jit(solution)/shard_map/deliver/pallas_call | solution.py:1004
